TPU v7x, 32 devices: a whole 2x2x4 slice. The times are simulated.
32 devices in a mesh: dp: 4 (over z), context: 8 (over y, x, core).
Axes of the slice: x: 2, y: 2, z: 4, core: 2. Of those that a mesh axis runs over, the one named last changes fastest.
Arguments:
- queries: bfloat16 [4, 1536, 4096], P('dp', 'context'), may hold values from -6 to 6
- key_rows: bfloat16 [4, 1536, 4096], P('dp', 'context'), may hold values from -6 to 6
- value_rows: bfloat16 [4, 1536, 4096], P('dp', 'context'), may hold values from -6 to 6
- out_grad: bfloat16 [4, 1536, 4096], P('dp', 'context'), may hold values from -6 to 6
- log_decay: float32 [4, 1536, 32], P('dp', 'context'), may hold values from -0.8 to 0
- norm_gain: float32 [4096], replicated, may hold values from 0.1 to 1.9
Outputs:
- query_grad: bfloat16 [4, 1536, 4096], P('dp', 'context')
- key_grad: bfloat16 [4, 1536, 4096], P('dp', 'context')
- value_grad: bfloat16 [4, 1536, 4096], P('dp', 'context')
- gain_grad: float32 [4096], P(('dp', 'context'))
All inputs are finite; a program needn't handle non-finite values.
Results may differ from a plain program's by a relative error of at most 0.0058.
Values sent between devices are 32-bit elements; how exact they have to be, the bound alone decides.
A program may use at most 128 MiB of HBM per device.

v0:
```python
import functools
import math

import jax
import jax.numpy as jnp
from jax import lax
from jax.experimental import pallas as pl
from jax.experimental.pallas import tpu as pltpu
from jax.sharding import PartitionSpec as P

EPSILON = 1e-06
F32 = jnp.float32
BF16 = jnp.bfloat16
LANES = 128
LAG = 3
LEAD = 2


def dot_nn(a, b):
    return lax.dot_general(a, b, (((1,), (0,)), ((), ())), preferred_element_type=F32)


def dot_nt(a, b):
    return lax.dot_general(a, b, (((1,), (1,)), ((), ())), preferred_element_type=F32)


def dot_tn(a, b):
    return lax.dot_general(a, b, (((0,), (0,)), ((), ())), preferred_element_type=F32)


def body(
    cfg,
    q_hbm, k_hbm, v_hbm, g_hbm, ld_ref, gain_ref,
    qg_hbm, kg_hbm, vg_hbm, gg_ref,
    q_ref, k_ref, v_ref, g_ref, qg_ref, kg_ref, vg_ref, in_sem, out_sem,
    cumc, cum_t, colb, att, vloc, fw, od_ref, acc_s, acc_p,
    gath, rows, coef, gp, gx, gy, gz,
    st_f, pr_f, tot_f, rx_f, sd_f, inc, pf_f,
    st_b, pr_b, tot_b, rx_b, sd_b, later, pf_b,
    ga_s, ga_r, gx_s, gx_r, gy_s, gy_r,
    d1s_f, d1r_f, xs_f, xr_f, d2s_f, d2r_f,
    d1s_b, d1r_b, xs_b, xr_b, d2s_b, d2r_b,
):
    n, n_dp, steps, heads = cfg["n"], cfg["n_dp"], cfg["steps"], cfg["heads"]
    half = heads // 2
    pos = q_ref.shape[0]
    feat = q_ref.shape[1]
    size = feat // heads
    width = feat // (n * n_dp)
    me = lax.axis_index("context")
    dp = lax.axis_index("dp")
    core = me % 2
    chip = me // 2
    mate = chip * 2 + (1 - core)

    barrier = pltpu.get_barrier_semaphore()
    for r in range(1, n):
        pl.semaphore_signal(barrier, inc=1, device_id={"context": (me + r) % n}, device_id_type=pl.DeviceIdType.MESH)
    for r in range(1, n_dp):
        pl.semaphore_signal(barrier, inc=1, device_id={"dp": (dp + r) % n_dp}, device_id_type=pl.DeviceIdType.MESH)

    loads = [
        pltpu.make_async_copy(src, dst, in_sem.at[i])
        for i, (src, dst) in enumerate(
            [(k_hbm, k_ref), (v_hbm, v_ref), (q_hbm, q_ref), (g_hbm, g_ref)]
        )
    ]
    for load in loads:
        load.start()

    def remote(src, dst, send, recv, **where):
        return pltpu.make_async_remote_copy(
            src_ref=src, dst_ref=dst, send_sem=send, recv_sem=recv,
            device_id=where, device_id_type=pl.DeviceIdType.MESH,
        )

    row_i = lax.broadcasted_iota(jnp.int32, (pos, pos), 0)
    col_i = lax.broadcasted_iota(jnp.int32, (pos, pos), 1)
    tri = jnp.where(row_i <= col_i, 1.0, 0.0).astype(F32)
    cum_t[...] = jnp.zeros_like(cum_t)
    cum_t[:heads, :] = lax.dot_general(
        ld_ref[...], tri, (((1,), (0,)), ((), ())),
        precision=lax.Precision.HIGHEST, preferred_element_type=F32,
    )
    cumc[...] = jnp.transpose(cum_t[...])
    cum = cumc[...]
    gath[me] = jnp.broadcast_to(cum[pos - 1 : pos, :], (8, LANES))
    pl.semaphore_wait(barrier, (n - 1) + (n_dp - 1))

    def gather_copy(r):
        return remote(gath.at[me], gath.at[me], ga_s.at[r], ga_r.at[r], context=(me + r) % n)

    def gather_wait(r):
        src = (me + n - r) % n
        return remote(gath.at[src], gath.at[src], ga_s.at[r], ga_r.at[r], context=(me + r) % n)

    for r in range(1, n):
        gather_copy(r).start()
    for h in range(heads):
        colb[h] = jnp.broadcast_to(cum[:, h : h + 1], (pos, LANES))
    loads[0].wait()
    loads[1].wait()

    def lanes(h):
        return pl.ds(pl.multiple_of(h * size, size), size)

    def column(h):
        return colb[h]

    def block_last(h):
        return colb[h, pos - 1 : pos, :]

    def decay_of(h):
        col = colb[h]
        wide = jnp.concatenate([col] * (-(-pos // LANES)), axis=1)[:, :pos]
        return jnp.exp(jnp.where(row_i >= col_i, wide - cum_t[pl.ds(h, 1), :], -jnp.inf))

    class Scan:
        def __init__(self, forward, st, pr, tot, rx, sd, result, pf, d1s, d1r, xs, xr, d2s, d2r):
            self.forward, self.st, self.pr, self.tot, self.rx = forward, st, pr, tot, rx
            self.sd, self.result, self.pf = sd, result, pf
            self.d1s, self.d1r, self.xs, self.xr, self.d2s, self.d2r = d1s, d1r, xs, xr, d2s, d2r
            self.first = (core == 0) if forward else (core == 1)
            self.base = 0 if forward else 6 + 3 * steps
            self.bits, self.partner, self.ups = [], [], []
            for s in range(steps):
                bit = (chip // (2**s)) % 2
                self.bits.append(bit)
                self.partner.append((chip + (1 - 2 * bit) * (2**s)) * 2 + core)
                self.ups.append((bit == 0) if forward else (bit == 1))

        def c(self, row, h):
            return coef[self.base + row, pl.ds(h, 1), :]

        def fill(self, last):
            ids = lax.broadcasted_iota(jnp.int32, last.shape, 0)
            chips = ids // 2

            def put(row, mask, keep=None):
                total = jnp.sum(jnp.where(mask, last, 0.0), axis=0, keepdims=True)
                value = jnp.exp(total)
                if keep is not None:
                    value = value * keep
                rows[self.base + row : self.base + row + 1, :] = value

            one = jnp.where(self.first, 1, 0)
            put(0, (ids == mate) & (one == 1))
            put(1, (ids == me) & (one == 0))
            put(2, (ids == mate) & (one == 0))
            put(3, (ids == me) & (one == 1))
            for s in range(steps):
                up = jnp.where(self.ups[s], 1, 0)
                mine = (chips // (2**s)) == (chip // (2**s))
                other = (chips // (2**s)) == ((self.partner[s] // 2) // (2**s))
                put(4 + 3 * s, other & (up == 1))
                put(5 + 3 * s, mine & (up == 0))
                ahead = (chips < chip) if self.forward else (chips > chip)
                put(6 + 3 * s, mine & ahead, keep=jnp.where(self.ups[s], 0.0, 1.0))
            if steps == 2:
                far, near = self.partner[1] // 2, self.partner[0] // 2

                def between(a, b):
                    return (chips > jnp.minimum(a, b)) & (chips < jnp.maximum(a, b))

                put(4 + 3 * steps, between(far, chip))
                put(5 + 3 * steps, between(far, near))

        def die1(self, k):
            return remote(self.st.at[(1 - core) * half + k], self.pr.at[k], self.d1s.at[k], self.d1r.at[k], context=mate)

        def link(self, s, k, slot=None):
            return remote(self.tot.at[s if slot is None else slot, k], self.rx.at[s, k], self.xs.at[s, k], self.xr.at[s, k], context=self.partner[s])

        def die2(self, k):
            return remote(self.sd.at[k], self.result.at[core * half + k], self.d2s.at[k], self.d2r.at[k], context=mate)

        def die2_in(self, k):
            return remote(self.sd.at[k], self.result.at[(1 - core) * half + k], self.d2s.at[k], self.d2r.at[k], context=mate)

        def send(self, s, k):
            if s < steps - 1:
                self.link(s, k).start()
            else:
                @pl.when(self.ups[s])
                def _():
                    self.link(s, k).start()

        def send_first(self, k):
            if steps != 2:
                self.send(0, k)
                return

            @pl.when(k % 2 == 0)
            def _():
                self.send(0, k)

            @pl.when((k % 2 == 1) & self.ups[1])
            def _():
                self.link(1, k, 0).start()

        def step(self, s, k):
            if steps != 2:
                self.stage(s, k)
                return
            h = core * half + k
            up0, up1 = self.ups[0], self.ups[1]
            down0, down1 = jnp.logical_not(up0), jnp.logical_not(up1)
            even, odd = k % 2 == 0, k % 2 == 1

            @pl.when(even)
            def _():
                self.stage(s, k)

            if s == 0:
                @pl.when(odd & up1 & up0)
                def _():
                    self.tot[1, k] = self.tot[0, k]
                    self.pf[k] = jnp.zeros_like(self.pf[k])

                @pl.when(odd & up1 & down0)
                def _():
                    self.pf[k] = jnp.zeros_like(self.pf[k])

                @pl.when(odd & down1)
                def _():
                    self.link(1, k, 0).wait_recv()
                    got = self.rx[1, k]
                    own = jnp.where(up0, 1.0, 0.0)
                    self.tot[1, k] = self.c(5 + 3 * steps, h) * got + own * self.tot[0, k]
                    self.pf[k] = self.c(4 + 3 * steps, h) * got

                @pl.when(odd & (up0 | down1))
                def _():
                    self.link(0, k, 1).start()
            else:
                @pl.when(odd & (down0 | down1))
                def _():
                    self.link(0, k, 1).wait_recv()
                    self.pf[k] = self.pf[k] + self.rx[0, k]

                @pl.when(odd)
                def _():
                    self.hand(k)

        def combine(self, k):
            h = core * half + k
            self.die1(k).wait_recv()
            self.tot[0, k] = self.c(0, h) * self.st[h] + self.c(1, h) * self.pr[k]
            self.send_first(k)

        def stage(self, s, k):
            h = core * half + k
            if s < steps - 1:
                self.link(s, k).wait_recv()
                got = self.rx[s, k]
                self.tot[s + 1, k] = self.c(4 + 3 * s, h) * self.tot[s, k] + self.c(5 + 3 * s, h) * got
                self.send(s + 1, k)
                part = self.c(6 + 3 * s, h) * got
                self.pf[k] = part if s == 0 else self.pf[k] + part
                return

            @pl.when(jnp.logical_not(self.ups[s]))
            def _():
                self.link(s, k).wait_recv()
                part = self.c(6 + 3 * s, h) * self.rx[s, k]
                self.pf[k] = part if s == 0 else self.pf[k] + part

            if s == 0:
                @pl.when(self.ups[s])
                def _():
                    self.pf[k] = jnp.zeros_like(self.pf[k])

            self.hand(k)

        def hand(self, k):
            h = core * half + k
            prefix = self.pf[k]
            head_first = jnp.where(self.first, 1.0, 0.0)
            self.sd[k] = self.c(3, h) * prefix + head_first * self.st[h]
            self.die2(k).start()
            self.result[h] = self.c(2, h) * prefix + (1.0 - head_first) * self.pr[k]

        def drain(self):
            def one(k, carry):
                self.die1(k).wait_send()
                self.die2(k).wait_send()
                even = (k % 2 == 0) | (steps != 2)

                @pl.when(even)
                def _():
                    for s in range(steps - 1):
                        self.link(s, k).wait_send()

                @pl.when(even & self.ups[steps - 1])
                def _():
                    self.link(steps - 1, k).wait_send()

                if steps == 2:
                    @pl.when((k % 2 == 1) & self.ups[1])
                    def _():
                        self.link(1, k, 0).wait_send()

                    @pl.when((k % 2 == 1) & (self.ups[0] | jnp.logical_not(self.ups[1])))
                    def _():
                        self.link(0, k, 1).wait_send()

                return carry

            lax.fori_loop(0, half, one, 0)

    fwd = Scan(True, st_f, pr_f, tot_f, rx_f, sd_f, inc, pf_f, d1s_f, d1r_f, xs_f, xr_f, d2s_f, d2r_f)
    bwd = Scan(False, st_b, pr_b, tot_b, rx_b, sd_b, later, pf_b, d1s_b, d1r_b, xs_b, xr_b, d2s_b, d2r_b)

    def guarded(k, run):
        @pl.when((k >= 0) & (k < half))
        def _():
            run(k)

    def own_state(h):
        shrink = jnp.exp(block_last(h) - column(h))
        late = (k_ref[:, lanes(h)].astype(F32) * shrink).astype(BF16)
        st_f[h] = dot_tn(late, v_ref[:, lanes(h)])

    def states(k):
        own_state((1 - core) * half + k)
        fwd.die1(k).start()
        own_state(core * half + k)

    def lead(k, carry):
        states(k)
        return carry

    lax.fori_loop(0, LEAD, lead, 0)
    for r in range(1, n):
        gather_wait(r).wait_recv()
    rows[...] = jnp.zeros_like(rows)
    last = gath[:, 0, :]
    fwd.fill(last)
    bwd.fill(last)
    turned = jnp.transpose(rows[...])
    for r in range(2 * (6 + 3 * steps)):
        coef[r] = jnp.broadcast_to(turned[:heads, r : r + 1], (heads, LANES))

    def rest(k, carry):
        guarded(k, states)
        fwd.combine(k - LEAD)
        return carry

    lax.fori_loop(LEAD, half + LEAD, rest, 0)
    acc_s[...] = jnp.zeros_like(acc_s)
    acc_p[...] = jnp.zeros_like(acc_p)

    def intra(h):
        s = dot_nt(q_ref[:, lanes(h)], k_ref[:, lanes(h)])
        w = (s * decay_of(h)).astype(BF16)
        fw[h] = w
        att[:, lanes(h)] = dot_nn(w, v_ref[:, lanes(h)])

    def scaled_of(h):
        return gain_ref[:, lanes(h)] * g_ref[:, lanes(h)].astype(F32)

    def inter(h):
        far = dot_nn(q_ref[:, lanes(h)], inc[h].astype(BF16))
        a = att[:, lanes(h)] + jnp.exp(column(h)) * far
        att[:, lanes(h)] = a
        acc_s[...] += a * a
        acc_p[...] += scaled_of(h) * a

    lags = [0, half] if steps == 2 else [LAG * s for s in range(steps)]
    lag_in = max(lags[-1] + LAG, half)

    def pass_loop(scan, local, finish, low=0, high=None):
        def one(it, carry):
            for s in range(steps):
                guarded(it - lags[s], functools.partial(scan.step, s))
            guarded(it, lambda k: local(core * half + k))
            guarded(it - half, lambda k: local((1 - core) * half + k))
            guarded(it - lags[-1], lambda k: finish(core * half + k))

            def arrived(k):
                scan.die2_in(k).wait_recv()
                finish((1 - core) * half + k)

            guarded(it - lag_in, arrived)
            return carry

        lax.fori_loop(low, half + lag_in if high is None else high, one, 0)

    loads[2].wait()
    loads[3].wait()
    pass_loop(fwd, intra, inter)

    mean_sq = jnp.sum(acc_s[...], axis=1, keepdims=True) * (1.0 / feat)
    inverse = lax.rsqrt(mean_sq + EPSILON)
    proj = inverse * (jnp.sum(acc_p[...], axis=1, keepdims=True) * (1.0 / feat))
    acc_s[...] = jnp.broadcast_to(inverse, acc_s.shape)
    acc_p[...] = jnp.broadcast_to(proj, acc_p.shape)

    def delta(h):
        inv = acc_s[...]
        normed = att[:, lanes(h)] * inv
        wide = g_ref[:, lanes(h)].astype(F32)
        scaled = gain_ref[:, lanes(h)] * wide
        od = (inv * (scaled - normed * acc_p[...])).astype(BF16)
        od_ref[:, lanes(h)] = od
        gp[:, lanes(h)] = jnp.sum((wide * normed).reshape(pos // 8, 8, size), axis=0)
        early = (q_ref[:, lanes(h)].astype(F32) * jnp.exp(column(h))).astype(BF16)
        st_b[h] = dot_tn(early, od)

    def deltas(k):
        delta((1 - core) * half + k)
        bwd.die1(k).start()
        delta(core * half + k)

    def back(k, carry):
        guarded(k, deltas)
        guarded(k - LEAD, bwd.combine)
        return carry

    lax.fori_loop(0, half + LEAD, back, 0)

    part = feat // n_dp

    def gx_copy(r):
        to = (dp + r) % n_dp
        return remote(gp.at[:, pl.ds(pl.multiple_of(to * part, LANES), part)], gx.at[r], gx_s.at[r], gx_r.at[r], dp=to)

    for r in range(1, n_dp):
        gx_copy(r).start()

    def put(src, dst, i, h):
        pltpu.make_async_copy(src.at[:, lanes(h)], dst.at[:, lanes(h)], out_sem.at[i]).start()

    def local_back(h):
        od = od_ref[:, lanes(h)]
        q = q_ref[:, lanes(h)]
        key = k_ref[:, lanes(h)]
        bw = (dot_nt(od, v_ref[:, lanes(h)]) * decay_of(h)).astype(BF16)
        far = dot_nt(od, inc[h].astype(BF16))
        qg_ref[:, lanes(h)] = (dot_nn(bw, key) + jnp.exp(column(h)) * far).astype(BF16)
        put(qg_ref, qg_hbm, 0, h)
        att[:, lanes(h)] = dot_tn(bw, q)
        vloc[:, lanes(h)] = dot_tn(fw[h], od)

    def finish_back(h):
        shrink = jnp.exp(block_last(h) - column(h))
        lt = later[h].astype(BF16)
        kg_ref[:, lanes(h)] = (att[:, lanes(h)] + shrink * dot_nt(v_ref[:, lanes(h)], lt)).astype(BF16)
        vg_ref[:, lanes(h)] = (vloc[:, lanes(h)] + shrink * dot_nn(k_ref[:, lanes(h)], lt)).astype(BF16)
        put(kg_ref, kg_hbm, 1, h)
        put(vg_ref, vg_hbm, 2, h)

    pass_loop(bwd, local_back, finish_back, 0, half // 2)
    for r in range(1, n_dp):
        gx_copy(r).wait_recv()
    total = gp[:, pl.ds(pl.multiple_of(dp * part, LANES), part)]
    for r in range(1, n_dp):
        total = total + gx[r]
    total = jnp.sum(total, axis=0, keepdims=True)
    for i in range(n):
        gy[i] = jnp.broadcast_to(total[:, i * width : (i + 1) * width], (8, width))

    def gy_copy(r):
        return remote(gy.at[(me + r) % n], gz.at[r], gy_s.at[r], gy_r.at[r], context=(me + r) % n)

    for r in range(1, n):
        gy_copy(r).start()

    pass_loop(bwd, local_back, finish_back, half // 2)

    out = gy[me]
    for r in range(1, n):
        gy_copy(r).wait_recv()
        out = out + gz[r]
    gg_ref[...] = out[0:1, :] * cfg["norm"]

    for r in range(1, n):
        gather_copy(r).wait_send()
        gy_copy(r).wait_send()
    for r in range(1, n_dp):
        gx_copy(r).wait_send()
    fwd.drain()
    bwd.drain()
    for i, (src, dst) in enumerate([(qg_ref, qg_hbm), (kg_ref, kg_hbm), (vg_ref, vg_hbm)]):
        pltpu.make_async_copy(src, dst, out_sem.at[i]).wait()


def settle(count, blocks, *refs):
    srcs, dsts, bufs = refs[:count], refs[count : 2 * count], refs[2 * count : 3 * count]
    in_sem, out_sem = refs[3 * count :]
    parts = [blocks if src.shape[0] % blocks == 0 else 1 for src in srcs]
    pieces = [(i, j) for i in range(count) for j in range(parts[i])]

    def copies(i, j):
        rows = srcs[i].shape[0] // parts[i]
        at = pl.ds(j * rows, rows)
        index = i * blocks + j
        return (
            pltpu.make_async_copy(srcs[i].at[at], bufs[i].at[at], in_sem.at[index]),
            pltpu.make_async_copy(bufs[i].at[at], dsts[i].at[at], out_sem.at[index]),
        )

    for i, j in pieces:
        copies(i, j)[0].start()
    for i, j in pieces:
        take, give = copies(i, j)
        take.wait()
        give.start()
    for i, j in pieces:
        copies(i, j)[1].wait()


def settled(arrays, blocks):
    count = len(arrays)
    anywhere = pl.BlockSpec(memory_space=pl.ANY)
    return pl.pallas_call(
        functools.partial(settle, count, blocks),
        out_shape=tuple(jax.ShapeDtypeStruct(a.shape, a.dtype) for a in arrays),
        in_specs=[anywhere] * count,
        out_specs=(anywhere,) * count,
        scratch_shapes=[
            *[pltpu.VMEM(a.shape, a.dtype) for a in arrays],
            pltpu.SemaphoreType.DMA((count * blocks,)),
            pltpu.SemaphoreType.DMA((count * blocks,)),
        ],
        compiler_params=pltpu.CompilerParams(vmem_limit_bytes=67043328),
    )(*arrays)


def per_device(queries, key_rows, value_rows, out_grad, log_decay, norm_gain):
    pos, feat = queries.shape[1:]
    heads = log_decay.shape[2]
    size = feat // heads
    half = heads // 2
    n, n_dp = lax.axis_size("context"), lax.axis_size("dp")
    steps = (n // 2).bit_length() - 1
    width = feat // (n * n_dp)
    cfg = dict(n=n, n_dp=n_dp, steps=steps, heads=heads, norm=1.0 / math.sqrt(pos * n * n_dp))
    vmem = pl.BlockSpec(memory_space=pltpu.VMEM)
    sem = pltpu.SemaphoreType.DMA

    def scan_buffers():
        return [
            pltpu.VMEM((heads, size, size), F32),
            pltpu.VMEM((half, size, size), F32),
            pltpu.VMEM((steps, half, size, size), F32),
            pltpu.VMEM((steps, half, size, size), F32),
            pltpu.VMEM((half, size, size), F32),
            pltpu.VMEM((heads, size, size), F32),
            pltpu.VMEM((half, size, size), F32),
        ]

    def scan_sems():
        return [sem((half,)), sem((half,)), sem((steps, half)), sem((steps, half)), sem((half,)), sem((half,))]

    rows_bf = pltpu.VMEM((pos, feat), BF16)
    scratch = [
        *([rows_bf] * 7), sem((4,)), sem((3,)),
        pltpu.VMEM((pos, LANES), F32),
        pltpu.VMEM((LANES, pos), F32),
        pltpu.VMEM((heads, pos, LANES), F32),
        pltpu.VMEM((pos, feat), F32),
        pltpu.VMEM((pos, feat), F32),
        pltpu.VMEM((heads, pos, pos), BF16),
        pltpu.VMEM((pos, feat), BF16),
        pltpu.VMEM((pos, LANES), F32),
        pltpu.VMEM((pos, LANES), F32),
        pltpu.VMEM((n, 8, LANES), F32),
        pltpu.VMEM((LANES, LANES), F32),
        pltpu.VMEM((2 * (6 + 3 * steps), heads, LANES), F32),
        pltpu.VMEM((8, feat), F32),
        pltpu.VMEM((n_dp, 8, feat // n_dp), F32),
        pltpu.VMEM((n, 8, width), F32),
        pltpu.VMEM((n, 8, width), F32),
        *scan_buffers(),
        *scan_buffers(),
        sem((n,)), sem((n,)), sem((n_dp,)), sem((n_dp,)), sem((n,)), sem((n,)),
        *scan_sems(),
        *scan_sems(),
    ]
    grid_out = jax.ShapeDtypeStruct((pos, feat), BF16)
    qg, kg, vg, gg = pl.pallas_call(
        functools.partial(body, cfg),
        out_shape=(grid_out, grid_out, grid_out, jax.ShapeDtypeStruct((1, width), F32)),
        in_specs=[pl.BlockSpec(memory_space=pl.ANY)] * 4 + [vmem] * 2,
        out_specs=(pl.BlockSpec(memory_space=pl.ANY),) * 3 + (vmem,),
        scratch_shapes=scratch,
        compiler_params=pltpu.CompilerParams(
            collective_id=0, has_side_effects=True, vmem_limit_bytes=67043328
        ),
    )(queries[0], key_rows[0], value_rows[0], out_grad[0], log_decay[0].T, norm_gain[None])
    qg, kg, vg, gg = settled((qg, kg, vg, gg), 4)
    return qg[None], kg[None], vg[None], gg[0]


def solution(mesh):
    rows = P("dp", "context", None)
    return jax.shard_map(
        per_device,
        mesh=mesh,
        in_specs=(rows,) * 5 + (P(),),
        out_specs=(rows, rows, rows, P(("dp", "context"))),
        check_vma=False,
    )
```

profile of v0, /device:TPU:0, one launch (start us, length us, event | category | flops | bytes accessed | tf_op | source)
XLA Modules:
  0.0 76.3 jit_solution(17678678335266329859)
XLA Ops:
  0.6 71.3 %shard_map.93 = (bf16[192,4096]{1,0:T(8,128)(2,1)}, bf16[192,4096]{1,0:T(8,128)(2,1)}, bf16[192,4096]{1,0:T(8,128)(2,1)}, f32[1,128]{1,0:T(1,128)}) custom-call(bf16[192,4096]{1,0:T(8,128)(2,1)} %bitcast.12, bf16[192,4096]{1,0:T(8,128)(2,1)} %bitcast.13, bf16[192,4096]{1,0:T(8,128)(2,1)} %bitcast.14, bf16[192,4096]{1,0:T(8,128)(2,1)} %bitcast.15, ...), custom_call_target="tpu_custom_call" | custom-call | tf_op jit(solution)/shard_map/pallas_call | solution.py:582
  71.9 4.3 %shard_map.94 = (bf16[192,4096]{1,0:T(8,128)(2,1)}, bf16[192,4096]{1,0:T(8,128)(2,1)}, bf16[192,4096]{1,0:T(8,128)(2,1)}, f32[1,128]{1,0:T(1,128)}) custom-call(bf16[192,4096]{1,0:T(8,128)(2,1)} %get-tuple-element.12.refs_0_, bf16[192,4096]{1,0:T(8,128)(2,1)} %get-tuple-element.13.refs_1_, bf16[192,4096]{1,0:T(8,128)(2,1)} %get-tuple-element.14.refs_2_, ...), custom_call_target="tpu_custom_call" | custom-call | tf_op jit(solution)/shard_map/pallas_call | solution.py:516
where the time goes:
time: 76.5 us; the launch traced here: 76.3 us
  Pallas kernels  75.7 us (99%)
    pallas_call x1, Pallas kernels, per_device(): pl.pallas_call(functools.partial(body, cfg), out_shape=(grid_out, grid_ou...  71.3 us
    pallas_call x1, Pallas kernels, settled(): pl.pallas_call(functools.partial(settle, count, blocks), out_shape=tuple(...  4.35 us

commit v1 on v0

--- a/solution.py
+++ b/solution.py
@@ -31,8 +31,8 @@
 def body(
     cfg,
     q_hbm, k_hbm, v_hbm, g_hbm, ld_ref, gain_ref,
-    qg_hbm, kg_hbm, vg_hbm, gg_ref,
-    q_ref, k_ref, v_ref, g_ref, qg_ref, kg_ref, vg_ref, in_sem, out_sem,
+    qg_ref, kg_ref, vg_ref, gg_ref,
+    q_ref, k_ref, v_ref, g_ref, in_sem,
     cumc, cum_t, colb, att, vloc, fw, od_ref, acc_s, acc_p,
     gath, rows, coef, gp, gx, gy, gz,
     st_f, pr_f, tot_f, rx_f, sd_f, inc, pf_f,
@@ -428,9 +428,6 @@
     for r in range(1, n_dp):
         gx_copy(r).start()
 
-    def put(src, dst, i, h):
-        pltpu.make_async_copy(src.at[:, lanes(h)], dst.at[:, lanes(h)], out_sem.at[i]).start()
-
     def local_back(h):
         od = od_ref[:, lanes(h)]
         q = q_ref[:, lanes(h)]
@@ -438,7 +435,6 @@
         bw = (dot_nt(od, v_ref[:, lanes(h)]) * decay_of(h)).astype(BF16)
         far = dot_nt(od, inc[h].astype(BF16))
         qg_ref[:, lanes(h)] = (dot_nn(bw, key) + jnp.exp(column(h)) * far).astype(BF16)
-        put(qg_ref, qg_hbm, 0, h)
         att[:, lanes(h)] = dot_tn(bw, q)
         vloc[:, lanes(h)] = dot_tn(fw[h], od)
 
@@ -447,8 +443,6 @@
         lt = later[h].astype(BF16)
         kg_ref[:, lanes(h)] = (att[:, lanes(h)] + shrink * dot_nt(v_ref[:, lanes(h)], lt)).astype(BF16)
         vg_ref[:, lanes(h)] = (vloc[:, lanes(h)] + shrink * dot_nn(k_ref[:, lanes(h)], lt)).astype(BF16)
-        put(kg_ref, kg_hbm, 1, h)
-        put(vg_ref, vg_hbm, 2, h)
 
     pass_loop(bwd, local_back, finish_back, 0, half // 2)
     for r in range(1, n_dp):
@@ -481,50 +475,27 @@
         gx_copy(r).wait_send()
     fwd.drain()
     bwd.drain()
-    for i, (src, dst) in enumerate([(qg_ref, qg_hbm), (kg_ref, kg_hbm), (vg_ref, vg_hbm)]):
-        pltpu.make_async_copy(src, dst, out_sem.at[i]).wait()
-
-
-def settle(count, blocks, *refs):
-    srcs, dsts, bufs = refs[:count], refs[count : 2 * count], refs[2 * count : 3 * count]
-    in_sem, out_sem = refs[3 * count :]
-    parts = [blocks if src.shape[0] % blocks == 0 else 1 for src in srcs]
-    pieces = [(i, j) for i in range(count) for j in range(parts[i])]
-
-    def copies(i, j):
-        rows = srcs[i].shape[0] // parts[i]
-        at = pl.ds(j * rows, rows)
-        index = i * blocks + j
-        return (
-            pltpu.make_async_copy(srcs[i].at[at], bufs[i].at[at], in_sem.at[index]),
-            pltpu.make_async_copy(bufs[i].at[at], dsts[i].at[at], out_sem.at[index]),
-        )
-
-    for i, j in pieces:
-        copies(i, j)[0].start()
-    for i, j in pieces:
-        take, give = copies(i, j)
-        take.wait()
-        give.start()
-    for i, j in pieces:
-        copies(i, j)[1].wait()
-
-
-def settled(arrays, blocks):
+
+
+def settle(count, *refs):
+    srcs, dsts, sems = refs[:count], refs[count : 2 * count], refs[2 * count]
+    copies = [pltpu.make_async_copy(srcs[i], dsts[i], sems.at[i]) for i in range(count)]
+    for copy in copies:
+        copy.start()
+    for copy in copies:
+        copy.wait()
+
+
+def settled(arrays):
     count = len(arrays)
-    anywhere = pl.BlockSpec(memory_space=pl.ANY)
     return pl.pallas_call(
-        functools.partial(settle, count, blocks),
+        functools.partial(settle, count),
         out_shape=tuple(jax.ShapeDtypeStruct(a.shape, a.dtype) for a in arrays),
-        in_specs=[anywhere] * count,
-        out_specs=(anywhere,) * count,
-        scratch_shapes=[
-            *[pltpu.VMEM(a.shape, a.dtype) for a in arrays],
-            pltpu.SemaphoreType.DMA((count * blocks,)),
-            pltpu.SemaphoreType.DMA((count * blocks,)),
-        ],
-        compiler_params=pltpu.CompilerParams(vmem_limit_bytes=67043328),
-    )(*arrays)
+        in_specs=[pl.BlockSpec(memory_space=pltpu.VMEM)] * count,
+        out_specs=(pl.BlockSpec(memory_space=pl.ANY),) * count,
+        scratch_shapes=[pltpu.SemaphoreType.DMA((count,))],
+        compiler_params=pltpu.CompilerParams(vmem_limit_bytes=1 << 20),
+    )(*[pltpu.with_memory_space_constraint(a, pltpu.VMEM) for a in arrays])
 
 
 def per_device(queries, key_rows, value_rows, out_grad, log_decay, norm_gain):
@@ -555,7 +526,7 @@
 
     rows_bf = pltpu.VMEM((pos, feat), BF16)
     scratch = [
-        *([rows_bf] * 7), sem((4,)), sem((3,)),
+        *([rows_bf] * 4), sem((4,)),
         pltpu.VMEM((pos, LANES), F32),
         pltpu.VMEM((LANES, pos), F32),
         pltpu.VMEM((heads, pos, LANES), F32),
@@ -578,18 +549,19 @@
         *scan_sems(),
         *scan_sems(),
     ]
-    grid_out = jax.ShapeDtypeStruct((pos, feat), BF16)
+    grid_out = pltpu.VMEM((pos, feat), BF16)
+    spare = 3 * pos * feat * 2 + (1 << 20)
     qg, kg, vg, gg = pl.pallas_call(
         functools.partial(body, cfg),
-        out_shape=(grid_out, grid_out, grid_out, jax.ShapeDtypeStruct((1, width), F32)),
+        out_shape=(grid_out, grid_out, grid_out, pltpu.VMEM((1, width), F32)),
         in_specs=[pl.BlockSpec(memory_space=pl.ANY)] * 4 + [vmem] * 2,
-        out_specs=(pl.BlockSpec(memory_space=pl.ANY),) * 3 + (vmem,),
+        out_specs=(vmem,) * 4,
         scratch_shapes=scratch,
         compiler_params=pltpu.CompilerParams(
-            collective_id=0, has_side_effects=True, vmem_limit_bytes=67043328
+            collective_id=0, has_side_effects=True, vmem_limit_bytes=67043328 - spare
         ),
     )(queries[0], key_rows[0], value_rows[0], out_grad[0], log_decay[0].T, norm_gain[None])
-    qg, kg, vg, gg = settled((qg, kg, vg, gg), 4)
+    qg, kg, vg, gg = settled((qg, kg, vg, gg))
     return qg[None], kg[None], vg[None], gg[0]
 
 

time: 76.5 us -> 73.8 us (0.965)
  Pallas kernels: 75.7 us -> 72.9 us
    pallas_call x1, Pallas kernels: 4.35 us -> 2.22 us  [settled(): pl.pallas_call(functools.partial(settle, count), out_shape=tuple((jax.Sha...]
where the time goes in v1:
time: 73.8 us; the launch traced here: 73.5 us
  Pallas kernels  72.9 us (99%)
    pallas_call x1, Pallas kernels, per_device(): pl.pallas_call(functools.partial(body, cfg), out_shape=(grid_out, grid_ou...  70.7 us
    pallas_call x1, Pallas kernels, settled(): pl.pallas_call(functools.partial(settle, count), out_shape=tuple((jax.Sha...  2.22 us

profile of v1, /device:TPU:0, one launch (start us, length us, event | category | flops | bytes accessed | tf_op | source)
XLA Modules:
  0.0 73.5 jit_solution(15956586433516843162)
XLA Ops:
  0.6 70.7 %shard_map.93 = (bf16[192,4096]{1,0:T(8,128)(2,1)S(1)}, bf16[192,4096]{1,0:T(8,128)(2,1)S(1)}, bf16[192,4096]{1,0:T(8,128)(2,1)S(1)}, f32[1,128]{1,0:T(1,128)S(1)}) custom-call(bf16[192,4096]{1,0:T(8,128)(2,1)} %bitcast.12, bf16[192,4096]{1,0:T(8,128)(2,1)} %bitcast.13, bf16[192,4096]{1,0:T(8,128)(2,1)} %bitcast.14, bf16[192,4096]{1,0:T(8,128)(2,1)} %bitcast.15, ...), custom_call_target="tpu_custom_call" | custom-call | tf_op jit(solution)/shard_map/pallas_call | solution.py:554
  71.3 2.2 %shard_map.94 = (bf16[192,4096]{1,0:T(8,128)(2,1)}, bf16[192,4096]{1,0:T(8,128)(2,1)}, bf16[192,4096]{1,0:T(8,128)(2,1)}, f32[1,128]{1,0:T(1,128)}) custom-call(bf16[192,4096]{1,0:T(8,128)(2,1)S(1)} %get-tuple-element.12.refs_0_, bf16[192,4096]{1,0:T(8,128)(2,1)S(1)} %get-tuple-element.13.refs_1_, bf16[192,4096]{1,0:T(8,128)(2,1)S(1)} %get-tuple-element.14.refs_2_, ...), custom_call_target="tpu_custom_call" | custom-call | tf_op jit(solution)/shard_map/pallas_call | solution.py:491

commit v2 on v1

--- a/solution.py
+++ b/solution.py
@@ -39,7 +39,7 @@
     st_b, pr_b, tot_b, rx_b, sd_b, later, pf_b,
     ga_s, ga_r, gx_s, gx_r, gy_s, gy_r,
     d1s_f, d1r_f, xs_f, xr_f, d2s_f, d2r_f,
-    d1s_b, d1r_b, xs_b, xr_b, d2s_b, d2r_b,
+    d1s_b, xs_b, xr_b, d2s_b,
 ):
     n, n_dp, steps, heads = cfg["n"], cfg["n_dp"], cfg["steps"], cfg["heads"]
     half = heads // 2
@@ -88,11 +88,11 @@
     pl.semaphore_wait(barrier, (n - 1) + (n_dp - 1))
 
     def gather_copy(r):
-        return remote(gath.at[me], gath.at[me], ga_s.at[r], ga_r.at[r], context=(me + r) % n)
-
-    def gather_wait(r):
-        src = (me + n - r) % n
-        return remote(gath.at[src], gath.at[src], ga_s.at[r], ga_r.at[r], context=(me + r) % n)
+        return remote(gath.at[me], gath.at[me], ga_s, ga_r, context=(me + r) % n)
+
+    def gather_all():
+        span = gath.at[pl.ds(0, n - 1)]
+        return remote(span, span, ga_s, ga_r, context=mate)
 
     for r in range(1, n):
         gather_copy(r).start()
@@ -166,16 +166,21 @@
                 put(5 + 3 * steps, between(far, near))
 
         def die1(self, k):
-            return remote(self.st.at[(1 - core) * half + k], self.pr.at[k], self.d1s.at[k], self.d1r.at[k], context=mate)
+            return remote(self.st.at[(1 - core) * half + k], self.pr.at[k], self.d1s, self.d1r.at[k], context=mate)
 
         def link(self, s, k, slot=None):
-            return remote(self.tot.at[s if slot is None else slot, k], self.rx.at[s, k], self.xs.at[s, k], self.xr.at[s, k], context=self.partner[s])
+            group = self.xs.at[steps if slot == 1 else s]
+            return remote(self.tot.at[s if slot is None else slot, k], self.rx.at[s, k], group, self.xr.at[s, k], context=self.partner[s])
+
+        def sent(self, group, count):
+            span = self.rx.at[0, pl.ds(0, count)]
+            return remote(span, span, self.xs.at[group], self.xr.at[0, 0], context=mate)
 
         def die2(self, k):
-            return remote(self.sd.at[k], self.result.at[core * half + k], self.d2s.at[k], self.d2r.at[k], context=mate)
+            return remote(self.sd.at[k], self.result.at[core * half + k], self.d2s, self.d2r.at[k], context=mate)
 
         def die2_in(self, k):
-            return remote(self.sd.at[k], self.result.at[(1 - core) * half + k], self.d2s.at[k], self.d2r.at[k], context=mate)
+            return remote(self.sd.at[k], self.result.at[(1 - core) * half + k], self.d2s, self.d2r.at[k], context=mate)
 
         def send(self, s, k):
             if s < steps - 1:
@@ -281,35 +286,29 @@
             self.result[h] = self.c(2, h) * prefix + (1.0 - head_first) * self.pr[k]
 
         def drain(self):
-            def one(k, carry):
-                self.die1(k).wait_send()
-                self.die2(k).wait_send()
-                even = (k % 2 == 0) | (steps != 2)
-
-                @pl.when(even)
-                def _():
-                    for s in range(steps - 1):
-                        self.link(s, k).wait_send()
-
-                @pl.when(even & self.ups[steps - 1])
-                def _():
-                    self.link(steps - 1, k).wait_send()
-
-                if steps == 2:
-                    @pl.when((k % 2 == 1) & self.ups[1])
-                    def _():
-                        self.link(1, k, 0).wait_send()
-
-                    @pl.when((k % 2 == 1) & (self.ups[0] | jnp.logical_not(self.ups[1])))
-                    def _():
-                        self.link(0, k, 1).wait_send()
-
-                return carry
-
-            lax.fori_loop(0, half, one, 0)
+            for group in (self.d1s, self.d2s):
+                remote(self.sd, self.sd, group, self.d1r.at[0], context=mate).wait_send()
+            if steps != 2:
+                for s in range(steps - 1):
+                    self.sent(s, half).wait_send()
+
+                @pl.when(self.ups[steps - 1])
+                def _():
+                    self.sent(steps - 1, half).wait_send()
+
+                return
+            self.sent(0, half // 2).wait_send()
+
+            @pl.when(self.ups[1])
+            def _():
+                self.sent(1, half).wait_send()
+
+            @pl.when(self.ups[0] | jnp.logical_not(self.ups[1]))
+            def _():
+                self.sent(2, half // 2).wait_send()
 
     fwd = Scan(True, st_f, pr_f, tot_f, rx_f, sd_f, inc, pf_f, d1s_f, d1r_f, xs_f, xr_f, d2s_f, d2r_f)
-    bwd = Scan(False, st_b, pr_b, tot_b, rx_b, sd_b, later, pf_b, d1s_b, d1r_b, xs_b, xr_b, d2s_b, d2r_b)
+    bwd = Scan(False, st_b, pr_b, tot_b, rx_b, sd_b, later, pf_b, d1s_b, d1r_f, xs_b, xr_b, d2s_b, d2r_f)
 
     def guarded(k, run):
         @pl.when((k >= 0) & (k < half))
@@ -331,8 +330,7 @@
         return carry
 
     lax.fori_loop(0, LEAD, lead, 0)
-    for r in range(1, n):
-        gather_wait(r).wait_recv()
+    gather_all().wait_recv()
     rows[...] = jnp.zeros_like(rows)
     last = gath[:, 0, :]
     fwd.fill(last)
@@ -423,7 +421,11 @@
 
     def gx_copy(r):
         to = (dp + r) % n_dp
-        return remote(gp.at[:, pl.ds(pl.multiple_of(to * part, LANES), part)], gx.at[r], gx_s.at[r], gx_r.at[r], dp=to)
+        return remote(gp.at[:, pl.ds(pl.multiple_of(to * part, LANES), part)], gx.at[r], gx_s, gx_r, dp=to)
+
+    def gx_all():
+        span = gx.at[pl.ds(1, n_dp - 1)]
+        return remote(span, span, gx_s, gx_r, dp=(dp + 1) % n_dp)
 
     for r in range(1, n_dp):
         gx_copy(r).start()
@@ -445,8 +447,8 @@
         vg_ref[:, lanes(h)] = (vloc[:, lanes(h)] + shrink * dot_nn(k_ref[:, lanes(h)], lt)).astype(BF16)
 
     pass_loop(bwd, local_back, finish_back, 0, half // 2)
-    for r in range(1, n_dp):
-        gx_copy(r).wait_recv()
+    if n_dp > 1:
+        gx_all().wait_recv()
     total = gp[:, pl.ds(pl.multiple_of(dp * part, LANES), part)]
     for r in range(1, n_dp):
         total = total + gx[r]
@@ -455,7 +457,11 @@
         gy[i] = jnp.broadcast_to(total[:, i * width : (i + 1) * width], (8, width))
 
     def gy_copy(r):
-        return remote(gy.at[(me + r) % n], gz.at[r], gy_s.at[r], gy_r.at[r], context=(me + r) % n)
+        return remote(gy.at[(me + r) % n], gz.at[r], gy_s, gy_r, context=(me + r) % n)
+
+    def gy_all():
+        span = gz.at[pl.ds(1, n - 1)]
+        return remote(span, span, gy_s, gy_r, context=mate)
 
     for r in range(1, n):
         gy_copy(r).start()
@@ -463,16 +469,15 @@
     pass_loop(bwd, local_back, finish_back, half // 2)
 
     out = gy[me]
+    gy_all().wait_recv()
     for r in range(1, n):
-        gy_copy(r).wait_recv()
         out = out + gz[r]
     gg_ref[...] = out[0:1, :] * cfg["norm"]
 
-    for r in range(1, n):
-        gather_copy(r).wait_send()
-        gy_copy(r).wait_send()
-    for r in range(1, n_dp):
-        gx_copy(r).wait_send()
+    gather_all().wait_send()
+    gy_all().wait_send()
+    if n_dp > 1:
+        gx_all().wait_send()
     fwd.drain()
     bwd.drain()
 
@@ -522,7 +527,7 @@
         ]
 
     def scan_sems():
-        return [sem((half,)), sem((half,)), sem((steps, half)), sem((steps, half)), sem((half,)), sem((half,))]
+        return [sem(()), sem((half,)), sem((steps + 1,)), sem((steps, half)), sem(()), sem((half,))]
 
     rows_bf = pltpu.VMEM((pos, feat), BF16)
     scratch = [
@@ -545,9 +550,9 @@
         pltpu.VMEM((n, 8, width), F32),
         *scan_buffers(),
         *scan_buffers(),
-        sem((n,)), sem((n,)), sem((n_dp,)), sem((n_dp,)), sem((n,)), sem((n,)),
+        *[sem(())] * 6,
         *scan_sems(),
-        *scan_sems(),
+        *[scan_sems()[i] for i in (0, 2, 3, 4)],
     ]
     grid_out = pltpu.VMEM((pos, feat), BF16)
     spare = 3 * pos * feat * 2 + (1 << 20)

time: 73.8 us -> 71.5 us (0.969)
  Pallas kernels: 72.9 us -> 70.7 us
    pallas_call x1, Pallas kernels: 70.7 us -> 68.4 us  [per_device(): pl.pallas_call(functools.partial(body, cfg), out_shape=(grid_out, grid_ou...]
where the time goes in v2:
time: 71.5 us; the launch traced here: 71.3 us
  Pallas kernels  70.7 us (99%)
    pallas_call x1, Pallas kernels, per_device(): pl.pallas_call(functools.partial(body, cfg), out_shape=(grid_out, grid_ou...  68.4 us
    pallas_call x1, Pallas kernels, settled(): pl.pallas_call(functools.partial(settle, count), out_shape=tuple((jax.Sha...  2.22 us

profile of v2, /device:TPU:0, one launch (start us, length us, event | category | flops | bytes accessed | tf_op | source)
XLA Modules:
  0.0 71.3 jit_solution(7363920073640705099)
XLA Ops:
  0.6 68.4 %shard_map.93 = (bf16[192,4096]{1,0:T(8,128)(2,1)S(1)}, bf16[192,4096]{1,0:T(8,128)(2,1)S(1)}, bf16[192,4096]{1,0:T(8,128)(2,1)S(1)}, f32[1,128]{1,0:T(1,128)S(1)}) custom-call(bf16[192,4096]{1,0:T(8,128)(2,1)} %bitcast.12, bf16[192,4096]{1,0:T(8,128)(2,1)} %bitcast.13, bf16[192,4096]{1,0:T(8,128)(2,1)} %bitcast.14, bf16[192,4096]{1,0:T(8,128)(2,1)} %bitcast.15, ...), custom_call_target="tpu_custom_call" | custom-call | tf_op jit(solution)/shard_map/pallas_call | solution.py:559
  69.1 2.2 %shard_map.94 = (bf16[192,4096]{1,0:T(8,128)(2,1)}, bf16[192,4096]{1,0:T(8,128)(2,1)}, bf16[192,4096]{1,0:T(8,128)(2,1)}, f32[1,128]{1,0:T(1,128)}) custom-call(bf16[192,4096]{1,0:T(8,128)(2,1)S(1)} %get-tuple-element.12.refs_0_, bf16[192,4096]{1,0:T(8,128)(2,1)S(1)} %get-tuple-element.13.refs_1_, bf16[192,4096]{1,0:T(8,128)(2,1)S(1)} %get-tuple-element.14.refs_2_, ...), custom_call_target="tpu_custom_call" | custom-call | tf_op jit(solution)/shard_map/pallas_call | solution.py:496

commit v3 on v2

--- a/solution.py
+++ b/solution.py
@@ -12,7 +12,7 @@
 F32 = jnp.float32
 BF16 = jnp.bfloat16
 LANES = 128
-LAG = 3
+LAG = 2
 LEAD = 2
 
 
@@ -65,7 +65,7 @@
             [(k_hbm, k_ref), (v_hbm, v_ref), (q_hbm, q_ref), (g_hbm, g_ref)]
         )
     ]
-    for load in loads:
+    for load in loads[:2]:
         load.start()
 
     def remote(src, dst, send, recv, **where):
@@ -96,10 +96,10 @@
 
     for r in range(1, n):
         gather_copy(r).start()
-    for h in range(heads):
-        colb[h] = jnp.broadcast_to(cum[:, h : h + 1], (pos, LANES))
     loads[0].wait()
     loads[1].wait()
+    loads[2].start()
+    loads[3].start()
 
     def lanes(h):
         return pl.ds(pl.multiple_of(h * size, size), size)
@@ -315,15 +315,25 @@
         def _():
             run(k)
 
-    def own_state(h):
-        shrink = jnp.exp(block_last(h) - column(h))
-        late = (k_ref[:, lanes(h)].astype(F32) * shrink).astype(BF16)
-        st_f[h] = dot_tn(late, v_ref[:, lanes(h)])
+    def own_states(hs):
+        made = []
+        for h in hs:
+            col = jnp.transpose(jnp.broadcast_to(cum_t[pl.ds(h, 1), :], (LANES, pos)))
+            shrink = jnp.exp(col[pos - 1 : pos, :] - col)
+            late = (k_ref[:, lanes(h)].astype(F32) * shrink).astype(BF16)
+            made.append((h, col, dot_tn(late, v_ref[:, lanes(h)])))
+        return made
+
+    def keep_state(made):
+        h, col, state = made
+        st_f[h] = state
+        colb[h] = col
 
     def states(k):
-        own_state((1 - core) * half + k)
+        far, near = own_states([(1 - core) * half + k, core * half + k])
+        keep_state(far)
         fwd.die1(k).start()
-        own_state(core * half + k)
+        keep_state(near)
 
     def lead(k, carry):
         states(k)
@@ -348,41 +358,74 @@
     acc_s[...] = jnp.zeros_like(acc_s)
     acc_p[...] = jnp.zeros_like(acc_p)
 
-    def intra(h):
-        s = dot_nt(q_ref[:, lanes(h)], k_ref[:, lanes(h)])
-        w = (s * decay_of(h)).astype(BF16)
-        fw[h] = w
-        att[:, lanes(h)] = dot_nn(w, v_ref[:, lanes(h)])
+    def intra(hs):
+        made = []
+        for h in hs:
+            s = dot_nt(q_ref[:, lanes(h)], k_ref[:, lanes(h)])
+            w = (s * decay_of(h)).astype(BF16)
+            made.append((h, w, dot_nn(w, v_ref[:, lanes(h)])))
+        for h, w, a in made:
+            fw[h] = w
+            att[:, lanes(h)] = a
 
     def scaled_of(h):
         return gain_ref[:, lanes(h)] * g_ref[:, lanes(h)].astype(F32)
 
-    def inter(h):
-        far = dot_nn(q_ref[:, lanes(h)], inc[h].astype(BF16))
-        a = att[:, lanes(h)] + jnp.exp(column(h)) * far
-        att[:, lanes(h)] = a
-        acc_s[...] += a * a
-        acc_p[...] += scaled_of(h) * a
-
-    lags = [0, half] if steps == 2 else [LAG * s for s in range(steps)]
-    lag_in = max(lags[-1] + LAG, half)
+    def inter(hs):
+        made = []
+        for h in hs:
+            far = dot_nn(q_ref[:, lanes(h)], inc[h].astype(BF16))
+            a = att[:, lanes(h)] + jnp.exp(column(h)) * far
+            made.append((h, a, scaled_of(h) * a))
+        square, cross = acc_s[...], acc_p[...]
+        for h, a, p in made:
+            square, cross = square + a * a, cross + p
+        acc_s[...], acc_p[...] = square, cross
+        for h, a, p in made:
+            att[:, lanes(h)] = a
+
+    unit = 2 if half % 2 == 0 else 1
+    count = half // unit
+    spread = -(-LAG // unit)
+    lags = [0, count] if steps == 2 else [spread * s for s in range(steps)]
+    lag_in = max(lags[-1] + spread, count)
+
+    def group(base):
+        return [base + i for i in range(unit)]
 
     def pass_loop(scan, local, finish, low=0, high=None):
         def one(it, carry):
             for s in range(steps):
-                guarded(it - lags[s], functools.partial(scan.step, s))
-            guarded(it, lambda k: local(core * half + k))
-            guarded(it - half, lambda k: local((1 - core) * half + k))
-            guarded(it - lags[-1], lambda k: finish(core * half + k))
-
-            def arrived(k):
-                scan.die2_in(k).wait_recv()
-                finish((1 - core) * half + k)
-
-            guarded(it - lag_in, arrived)
+                at = it - lags[s]
+
+                @pl.when((at >= 0) & (at < count))
+                def _():
+                    for k in group(at * unit):
+                        scan.step(s, k)
+
+            @pl.when(it < 2 * count)
+            def _():
+                late = it // count
+                who = core + late * (1 - 2 * core)
+                local(group(who * half + (it - late * count) * unit))
+
+            own = it - lags[-1]
+
+            @pl.when((own >= 0) & (own < count))
+            def _():
+                finish(group(core * half + own * unit))
+
+            come = it - lag_in
+
+            @pl.when((come >= 0) & (come < count))
+            def _():
+                for k in group(come * unit):
+                    scan.die2_in(k).wait_recv()
+                finish(group((1 - core) * half + come * unit))
+
             return carry
 
-        lax.fori_loop(low, half + lag_in if high is None else high, one, 0)
+        lax.fori_loop(low, count + lag_in if high is None else high, one, 0)
 
     loads[2].wait()
     loads[3].wait()
@@ -400,15 +443,21 @@
         wide = g_ref[:, lanes(h)].astype(F32)
         scaled = gain_ref[:, lanes(h)] * wide
         od = (inv * (scaled - normed * acc_p[...])).astype(BF16)
+        terms = jnp.sum((wide * normed).reshape(pos // 8, 8, size), axis=0)
+        early = (q_ref[:, lanes(h)].astype(F32) * jnp.exp(column(h))).astype(BF16)
+        return h, od, terms, dot_tn(early, od)
+
+    def keep_delta(made):
+        h, od, terms, state = made
+        st_b[h] = state
         od_ref[:, lanes(h)] = od
-        gp[:, lanes(h)] = jnp.sum((wide * normed).reshape(pos // 8, 8, size), axis=0)
-        early = (q_ref[:, lanes(h)].astype(F32) * jnp.exp(column(h))).astype(BF16)
-        st_b[h] = dot_tn(early, od)
+        gp[:, lanes(h)] = terms
 
     def deltas(k):
-        delta((1 - core) * half + k)
+        far, near = delta((1 - core) * half + k), delta(core * half + k)
+        keep_delta(far)
         bwd.die1(k).start()
-        delta(core * half + k)
+        keep_delta(near)
 
     def back(k, carry):
         guarded(k, deltas)
@@ -430,23 +479,34 @@
     for r in range(1, n_dp):
         gx_copy(r).start()
 
-    def local_back(h):
-        od = od_ref[:, lanes(h)]
-        q = q_ref[:, lanes(h)]
-        key = k_ref[:, lanes(h)]
-        bw = (dot_nt(od, v_ref[:, lanes(h)]) * decay_of(h)).astype(BF16)
-        far = dot_nt(od, inc[h].astype(BF16))
-        qg_ref[:, lanes(h)] = (dot_nn(bw, key) + jnp.exp(column(h)) * far).astype(BF16)
-        att[:, lanes(h)] = dot_tn(bw, q)
-        vloc[:, lanes(h)] = dot_tn(fw[h], od)
-
-    def finish_back(h):
-        shrink = jnp.exp(block_last(h) - column(h))
-        lt = later[h].astype(BF16)
-        kg_ref[:, lanes(h)] = (att[:, lanes(h)] + shrink * dot_nt(v_ref[:, lanes(h)], lt)).astype(BF16)
-        vg_ref[:, lanes(h)] = (vloc[:, lanes(h)] + shrink * dot_nn(k_ref[:, lanes(h)], lt)).astype(BF16)
-
-    pass_loop(bwd, local_back, finish_back, 0, half // 2)
+    def local_back(hs):
+        made = []
+        for h in hs:
+            od = od_ref[:, lanes(h)]
+            q = q_ref[:, lanes(h)]
+            key = k_ref[:, lanes(h)]
+            bw = (dot_nt(od, v_ref[:, lanes(h)]) * decay_of(h)).astype(BF16)
+            far = dot_nt(od, inc[h].astype(BF16))
+            qg = (dot_nn(bw, key) + jnp.exp(column(h)) * far).astype(BF16)
+            made.append((h, qg, dot_tn(bw, q), dot_tn(fw[h], od)))
+        for h, qg, kl, vl in made:
+            qg_ref[:, lanes(h)] = qg
+            att[:, lanes(h)] = kl
+            vloc[:, lanes(h)] = vl
+
+    def finish_back(hs):
+        made = []
+        for h in hs:
+            shrink = jnp.exp(block_last(h) - column(h))
+            lt = later[h].astype(BF16)
+            kg = att[:, lanes(h)] + shrink * dot_nt(v_ref[:, lanes(h)], lt)
+            vg = vloc[:, lanes(h)] + shrink * dot_nn(k_ref[:, lanes(h)], lt)
+            made.append((h, kg.astype(BF16), vg.astype(BF16)))
+        for h, kg, vg in made:
+            kg_ref[:, lanes(h)] = kg
+            vg_ref[:, lanes(h)] = vg
+
+    pass_loop(bwd, local_back, finish_back, 0, count // 2)
     if n_dp > 1:
         gx_all().wait_recv()
     total = gp[:, pl.ds(pl.multiple_of(dp * part, LANES), part)]
@@ -466,7 +526,7 @@
     for r in range(1, n):
         gy_copy(r).start()
 
-    pass_loop(bwd, local_back, finish_back, half // 2)
+    pass_loop(bwd, local_back, finish_back, count // 2)
 
     out = gy[me]
     gy_all().wait_recv()

time: 71.5 us -> 69.2 us (0.968)
  Pallas kernels: 70.7 us -> 68.3 us
    pallas_call x1, Pallas kernels: 68.4 us -> 66.1 us  [per_device(): pl.pallas_call(functools.partial(body, cfg), out_shape=(grid_out, grid_ou...]
where the time goes in v3:
time: 69.2 us; the launch traced here: 68.9 us
  Pallas kernels  68.3 us (99%)
    pallas_call x1, Pallas kernels, per_device(): pl.pallas_call(functools.partial(body, cfg), out_shape=(grid_out, grid_ou...  66.1 us
    pallas_call x1, Pallas kernels, settled(): pl.pallas_call(functools.partial(settle, count), out_shape=tuple((jax.Sha...  2.22 us

profile of v3, /device:TPU:0, one launch (start us, length us, event | category | flops | bytes accessed | tf_op | source)
XLA Modules:
  0.0 68.9 jit_solution(13125494679700576793)
XLA Ops:
  0.6 66.1 %shard_map.93 = (bf16[192,4096]{1,0:T(8,128)(2,1)S(1)}, bf16[192,4096]{1,0:T(8,128)(2,1)S(1)}, bf16[192,4096]{1,0:T(8,128)(2,1)S(1)}, f32[1,128]{1,0:T(1,128)S(1)}) custom-call(bf16[192,4096]{1,0:T(8,128)(2,1)} %bitcast.12, bf16[192,4096]{1,0:T(8,128)(2,1)} %bitcast.13, bf16[192,4096]{1,0:T(8,128)(2,1)} %bitcast.14, bf16[192,4096]{1,0:T(8,128)(2,1)} %bitcast.15, ...), custom_call_target="tpu_custom_call" | custom-call | tf_op jit(solution)/shard_map/pallas_call | solution.py:619
  66.7 2.2 %shard_map.94 = (bf16[192,4096]{1,0:T(8,128)(2,1)}, bf16[192,4096]{1,0:T(8,128)(2,1)}, bf16[192,4096]{1,0:T(8,128)(2,1)}, f32[1,128]{1,0:T(1,128)}) custom-call(bf16[192,4096]{1,0:T(8,128)(2,1)S(1)} %get-tuple-element.12.refs_0_, bf16[192,4096]{1,0:T(8,128)(2,1)S(1)} %get-tuple-element.13.refs_1_, bf16[192,4096]{1,0:T(8,128)(2,1)S(1)} %get-tuple-element.14.refs_2_, ...), custom_call_target="tpu_custom_call" | custom-call | tf_op jit(solution)/shard_map/pallas_call | solution.py:556

commit v4 on v3

--- a/solution.py
+++ b/solution.py
@@ -37,7 +37,7 @@
     gath, rows, coef, gp, gx, gy, gz,
     st_f, pr_f, tot_f, rx_f, sd_f, inc, pf_f,
     st_b, pr_b, tot_b, rx_b, sd_b, later, pf_b,
-    ga_s, ga_r, gx_s, gx_r, gy_s, gy_r,
+    entry, ga_s, ga_r, gx_s, gx_r, gy_s, gy_r, gz_s, gz_r,
     d1s_f, d1r_f, xs_f, xr_f, d2s_f, d2r_f,
     d1s_b, xs_b, xr_b, d2s_b,
 ):
@@ -53,11 +53,20 @@
     chip = me // 2
     mate = chip * 2 + (1 - core)
 
+    lead_of = n - 1
+    leads = me == lead_of
     barrier = pltpu.get_barrier_semaphore()
     for r in range(1, n):
-        pl.semaphore_signal(barrier, inc=1, device_id={"context": (me + r) % n}, device_id_type=pl.DeviceIdType.MESH)
+        peer = (me + r) % n
+
+        @pl.when(peer != lead_of)
+        def _():
+            pl.semaphore_signal(barrier, inc=1, device_id={"context": peer}, device_id_type=pl.DeviceIdType.MESH)
+
     for r in range(1, n_dp):
-        pl.semaphore_signal(barrier, inc=1, device_id={"dp": (dp + r) % n_dp}, device_id_type=pl.DeviceIdType.MESH)
+        @pl.when(leads)
+        def _():
+            pl.semaphore_signal(barrier, inc=1, device_id={"dp": (dp + r) % n_dp}, device_id_type=pl.DeviceIdType.MESH)
 
     loads = [
         pltpu.make_async_copy(src, dst, in_sem.at[i])
@@ -85,7 +94,18 @@
     cumc[...] = jnp.transpose(cum_t[...])
     cum = cumc[...]
     gath[me] = jnp.broadcast_to(cum[pos - 1 : pos, :], (8, LANES))
-    pl.semaphore_wait(barrier, (n - 1) + (n_dp - 1))
+
+    @pl.when(jnp.logical_not(leads))
+    def _():
+        pl.semaphore_wait(barrier, n - 1)
+
+    @pl.when(me == lead_of - 1)
+    def _():
+        pl.semaphore_signal(entry, inc=1, device_id={"context": lead_of}, device_id_type=pl.DeviceIdType.MESH)
+
+    @pl.when(leads)
+    def _():
+        pl.semaphore_wait(entry, 1)
 
     def gather_copy(r):
         return remote(gath.at[me], gath.at[me], ga_s, ga_r, context=(me + r) % n)
@@ -393,7 +413,7 @@
     def group(base):
         return [base + i for i in range(unit)]
 
-    def pass_loop(scan, local, finish, low=0, high=None):
+    def pass_loop(scan, local, finish, extra=None):
         def one(it, carry):
             for s in range(steps):
                 at = it - lags[s]
@@ -409,6 +429,9 @@
                 who = core + late * (1 - 2 * core)
                 local(group(who * half + (it - late * count) * unit))
 
+            if extra is not None:
+                extra(it)
+
             own = it - lags[-1]
 
             @pl.when((own >= 0) & (own < count))
@@ -425,7 +448,7 @@
 
             return carry
 
-        lax.fori_loop(low, count + lag_in if high is None else high, one, 0)
+        lax.fori_loop(0, count + lag_in, one, 0)
 
     loads[2].wait()
     loads[3].wait()
@@ -443,7 +466,7 @@
         wide = g_ref[:, lanes(h)].astype(F32)
         scaled = gain_ref[:, lanes(h)] * wide
         od = (inv * (scaled - normed * acc_p[...])).astype(BF16)
-        terms = jnp.sum((wide * normed).reshape(pos // 8, 8, size), axis=0)
+        terms = jnp.sum(wide * normed, axis=0, keepdims=True)
         early = (q_ref[:, lanes(h)].astype(F32) * jnp.exp(column(h))).astype(BF16)
         return h, od, terms, dot_tn(early, od)
 
@@ -468,16 +491,56 @@
 
     part = feat // n_dp
 
-    def gx_copy(r):
+    def gain_in():
+        return remote(gp, gx.at[me], gx_s, gx_r, context=lead_of)
+
+    def gain_in_all():
+        span = gx.at[pl.ds(0, n - 1)]
+        return remote(span, span, gx_s, gx_r, context=lead_of - 1)
+
+    def gain_across(r):
         to = (dp + r) % n_dp
-        return remote(gp.at[:, pl.ds(pl.multiple_of(to * part, LANES), part)], gx.at[r], gx_s, gx_r, dp=to)
-
-    def gx_all():
-        span = gx.at[pl.ds(1, n_dp - 1)]
-        return remote(span, span, gx_s, gx_r, dp=(dp + 1) % n_dp)
-
-    for r in range(1, n_dp):
-        gx_copy(r).start()
+        return remote(gp.at[:, pl.ds(pl.multiple_of(to * part, LANES), part)], gz.at[r], gy_s, gy_r, dp=to)
+
+    def gain_across_all():
+        span = gz.at[pl.ds(1, n_dp - 1)]
+        return remote(span, span, gy_s, gy_r, dp=(dp + 1) % n_dp)
+
+    def gain_out(i):
+        return remote(gy.at[i], gy.at[lead_of], gz_s, gz_r, context=i)
+
+    def gain_out_all():
+        span = gy.at[pl.ds(0, n - 1)]
+        return remote(span, span, gz_s, gz_r, context=lead_of - 1)
+
+    @pl.when(jnp.logical_not(leads))
+    def _():
+        gain_in().start()
+
+    def gain_step(it):
+        @pl.when(leads & (it == count // 2))
+        def _():
+            gain_in_all().wait_recv()
+            total = gp[...]
+            for r in range(n - 1):
+                total = total + gx[r]
+            gp[...] = total
+            if n_dp > 1:
+                pl.semaphore_wait(barrier, n_dp - 1)
+                for r in range(1, n_dp):
+                    gain_across(r).start()
+
+        @pl.when(leads & (it == count))
+        def _():
+            total = gp[:, pl.ds(pl.multiple_of(dp * part, LANES), part)]
+            if n_dp > 1:
+                gain_across_all().wait_recv()
+                for r in range(1, n_dp):
+                    total = total + gz[r]
+            for i in range(n):
+                gy[i] = jnp.broadcast_to(total[:, i * width : (i + 1) * width], (8, width))
+            for i in range(n - 1):
+                gain_out(i).start()
 
     def local_back(hs):
         made = []
@@ -506,38 +569,21 @@
             kg_ref[:, lanes(h)] = kg
             vg_ref[:, lanes(h)] = vg
 
-    pass_loop(bwd, local_back, finish_back, 0, count // 2)
-    if n_dp > 1:
-        gx_all().wait_recv()
-    total = gp[:, pl.ds(pl.multiple_of(dp * part, LANES), part)]
-    for r in range(1, n_dp):
-        total = total + gx[r]
-    total = jnp.sum(total, axis=0, keepdims=True)
-    for i in range(n):
-        gy[i] = jnp.broadcast_to(total[:, i * width : (i + 1) * width], (8, width))
-
-    def gy_copy(r):
-        return remote(gy.at[(me + r) % n], gz.at[r], gy_s, gy_r, context=(me + r) % n)
-
-    def gy_all():
-        span = gz.at[pl.ds(1, n - 1)]
-        return remote(span, span, gy_s, gy_r, context=mate)
-
-    for r in range(1, n):
-        gy_copy(r).start()
-
-    pass_loop(bwd, local_back, finish_back, count // 2)
-
-    out = gy[me]
-    gy_all().wait_recv()
-    for r in range(1, n):
-        out = out + gz[r]
-    gg_ref[...] = out[0:1, :] * cfg["norm"]
-
+    pass_loop(bwd, local_back, finish_back, gain_step)
+
+    @pl.when(jnp.logical_not(leads))
+    def _():
+        gain_out(0).wait_recv()
+        gain_in().wait_send()
+
+    @pl.when(leads)
+    def _():
+        gain_out_all().wait_send()
+        if n_dp > 1:
+            gain_across_all().wait_send()
+
+    gg_ref[...] = gy[lead_of][0:1, :] * cfg["norm"]
     gather_all().wait_send()
-    gy_all().wait_send()
-    if n_dp > 1:
-        gx_all().wait_send()
     fwd.drain()
     bwd.drain()
 
@@ -604,13 +650,13 @@
         pltpu.VMEM((n, 8, LANES), F32),
         pltpu.VMEM((LANES, LANES), F32),
         pltpu.VMEM((2 * (6 + 3 * steps), heads, LANES), F32),
-        pltpu.VMEM((8, feat), F32),
-        pltpu.VMEM((n_dp, 8, feat // n_dp), F32),
+        pltpu.VMEM((1, feat), F32),
+        pltpu.VMEM((n - 1, 1, feat), F32),
         pltpu.VMEM((n, 8, width), F32),
-        pltpu.VMEM((n, 8, width), F32),
+        pltpu.VMEM((n_dp, 1, feat // n_dp), F32),
         *scan_buffers(),
         *scan_buffers(),
-        *[sem(())] * 6,
+        pltpu.SemaphoreType.REGULAR(()), *[sem(())] * 8,
         *scan_sems(),
         *[scan_sems()[i] for i in (0, 2, 3, 4)],
     ]

time: 69.2 us -> 66.4 us (0.960)
  Pallas kernels: 68.3 us -> 65.5 us
    pallas_call x1, Pallas kernels: 66.1 us -> 63.3 us  [per_device(): pl.pallas_call(functools.partial(body, cfg), out_shape=(grid_out, grid_ou...]
where the time goes in v4:
time: 66.4 us; the launch traced here: 66.2 us
  Pallas kernels  65.5 us (99%)
    pallas_call x1, Pallas kernels, per_device(): pl.pallas_call(functools.partial(body, cfg), out_shape=(grid_out, grid_ou...  63.3 us
    pallas_call x1, Pallas kernels, settled(): pl.pallas_call(functools.partial(settle, count), out_shape=tuple((jax.Sha...  2.22 us

profile of v4, /device:TPU:0, one launch (start us, length us, event | category | flops | bytes accessed | tf_op | source)
XLA Modules:
  0.0 66.2 jit_solution(12456778534705814162)
XLA Ops:
  0.6 63.3 %shard_map.93 = (bf16[192,4096]{1,0:T(8,128)(2,1)S(1)}, bf16[192,4096]{1,0:T(8,128)(2,1)S(1)}, bf16[192,4096]{1,0:T(8,128)(2,1)S(1)}, f32[1,128]{1,0:T(1,128)S(1)}) custom-call(bf16[192,4096]{1,0:T(8,128)(2,1)} %bitcast.12, bf16[192,4096]{1,0:T(8,128)(2,1)} %bitcast.13, bf16[192,4096]{1,0:T(8,128)(2,1)} %bitcast.14, bf16[192,4096]{1,0:T(8,128)(2,1)} %bitcast.15, ...), custom_call_target="tpu_custom_call" | custom-call | tf_op jit(solution)/shard_map/pallas_call | solution.py:665
  64.0 2.2 %shard_map.94 = (bf16[192,4096]{1,0:T(8,128)(2,1)}, bf16[192,4096]{1,0:T(8,128)(2,1)}, bf16[192,4096]{1,0:T(8,128)(2,1)}, f32[1,128]{1,0:T(1,128)}) custom-call(bf16[192,4096]{1,0:T(8,128)(2,1)S(1)} %get-tuple-element.12.refs_0_, bf16[192,4096]{1,0:T(8,128)(2,1)S(1)} %get-tuple-element.13.refs_1_, bf16[192,4096]{1,0:T(8,128)(2,1)S(1)} %get-tuple-element.14.refs_2_, ...), custom_call_target="tpu_custom_call" | custom-call | tf_op jit(solution)/shard_map/pallas_call | solution.py:602

commit v5 on v4

--- a/solution.py
+++ b/solution.py
@@ -14,6 +14,7 @@
 LANES = 128
 LAG = 2
 LEAD = 2
+SOLO = 6
 
 
 def dot_nn(a, b):
@@ -30,14 +31,14 @@
 
 def body(
     cfg,
-    q_hbm, k_hbm, v_hbm, g_hbm, ld_ref, gain_ref,
+    q_hbm, k_hbm, v_hbm, g_hbm, ld_hbm, gain_hbm,
     qg_ref, kg_ref, vg_ref, gg_ref,
-    q_ref, k_ref, v_ref, g_ref, in_sem,
+    q_ref, k_ref, v_ref, g_ref, ld_ref, gain_ref, in_sem,
     cumc, cum_t, colb, att, vloc, fw, od_ref, acc_s, acc_p,
     gath, rows, coef, gp, gx, gy, gz,
     st_f, pr_f, tot_f, rx_f, sd_f, inc, pf_f,
     st_b, pr_b, tot_b, rx_b, sd_b, later, pf_b,
-    entry, ga_s, ga_r, gx_s, gx_r, gy_s, gy_r, gz_s, gz_r,
+    entry, gm_s, gm_r, ga_s, ga_r, gx_s, gx_r, gy_s, gy_r, gz_s, gz_r,
     d1s_f, d1r_f, xs_f, xr_f, d2s_f, d2r_f,
     d1s_b, xs_b, xr_b, d2s_b,
 ):
@@ -53,6 +54,29 @@
     chip = me // 2
     mate = chip * 2 + (1 - core)
 
+    fetch = [
+        pltpu.make_async_copy(src, dst, in_sem.at[i])
+        for i, (src, dst) in enumerate(
+            [(ld_hbm, ld_ref), (q_hbm, q_ref), (g_hbm, g_ref), (gain_hbm, gain_ref)]
+        )
+    ]
+    fetch[0].start()
+    head_start = max(1, half // 4)
+
+    def columns(src, dst, low, high, i):
+        for side in (1 - core, core):
+            at = pl.ds(pl.multiple_of((side * half + low) * size, LANES), (high - low) * size)
+            pltpu.make_async_copy(src.at[:, at], dst.at[:, at], in_sem.at[i]).start()
+
+    def columns_wait(src, dst, low, high, i):
+        at = pl.ds(0, 2 * (high - low) * size)
+        pltpu.make_async_copy(src.at[:, at], dst.at[:, at], in_sem.at[i]).wait()
+
+    columns(k_hbm, k_ref, 0, head_start, 4)
+    columns(v_hbm, v_ref, 0, head_start, 5)
+    columns(k_hbm, k_ref, head_start, half, 6)
+    columns(v_hbm, v_ref, head_start, half, 7)
+
     lead_of = n - 1
     leads = me == lead_of
     barrier = pltpu.get_barrier_semaphore()
@@ -68,15 +92,6 @@
         def _():
             pl.semaphore_signal(barrier, inc=1, device_id={"dp": (dp + r) % n_dp}, device_id_type=pl.DeviceIdType.MESH)
 
-    loads = [
-        pltpu.make_async_copy(src, dst, in_sem.at[i])
-        for i, (src, dst) in enumerate(
-            [(k_hbm, k_ref), (v_hbm, v_ref), (q_hbm, q_ref), (g_hbm, g_ref)]
-        )
-    ]
-    for load in loads[:2]:
-        load.start()
-
     def remote(src, dst, send, recv, **where):
         return pltpu.make_async_remote_copy(
             src_ref=src, dst_ref=dst, send_sem=send, recv_sem=recv,
@@ -87,6 +102,7 @@
     col_i = lax.broadcasted_iota(jnp.int32, (pos, pos), 1)
     tri = jnp.where(row_i <= col_i, 1.0, 0.0).astype(F32)
     cum_t[...] = jnp.zeros_like(cum_t)
+    fetch[0].wait()
     cum_t[:heads, :] = lax.dot_general(
         ld_ref[...], tri, (((1,), (0,)), ((), ())),
         precision=lax.Precision.HIGHEST, preferred_element_type=F32,
@@ -110,16 +126,21 @@
     def gather_copy(r):
         return remote(gath.at[me], gath.at[me], ga_s, ga_r, context=(me + r) % n)
 
+    def gather_mate():
+        return remote(gath.at[me], gath.at[me], gm_s, gm_r, context=mate)
+
     def gather_all():
-        span = gath.at[pl.ds(0, n - 1)]
+        span = gath.at[pl.ds(0, n - 2)]
         return remote(span, span, ga_s, ga_r, context=mate)
 
+    gather_mate().start()
     for r in range(1, n):
-        gather_copy(r).start()
-    loads[0].wait()
-    loads[1].wait()
-    loads[2].start()
-    loads[3].start()
+        @pl.when((me + r) % n != mate)
+        def _():
+            gather_copy(r).start()
+
+    columns_wait(k_hbm, k_ref, 0, head_start, 4)
+    columns_wait(v_hbm, v_ref, 0, head_start, 5)
 
     def lanes(h):
         return pl.ds(pl.multiple_of(h * size, size), size)
@@ -152,6 +173,12 @@
         def c(self, row, h):
             return coef[self.base + row, pl.ds(h, 1), :]
 
+        def fill_near(self, mine, other):
+            one = jnp.where(self.first, 1.0, 0.0)
+            values = [one * other, (1.0 - one) * mine, (1.0 - one) * other, one * mine]
+            for row, total in enumerate(values):
+                rows[self.base + row : self.base + row + 1, :] = jnp.exp(total)
+
         def fill(self, last):
             ids = lax.broadcasted_iota(jnp.int32, last.shape, 0)
             chips = ids // 2
@@ -163,11 +190,6 @@
                     value = value * keep
                 rows[self.base + row : self.base + row + 1, :] = value
 
-            one = jnp.where(self.first, 1, 0)
-            put(0, (ids == mate) & (one == 1))
-            put(1, (ids == me) & (one == 0))
-            put(2, (ids == mate) & (one == 0))
-            put(3, (ids == me) & (one == 1))
             for s in range(steps):
                 up = jnp.where(self.ups[s], 1, 0)
                 mine = (chips // (2**s)) == (chip // (2**s))
@@ -360,23 +382,47 @@
         return carry
 
     lax.fori_loop(0, LEAD, lead, 0)
-    gather_all().wait_recv()
+    gather_mate().wait_recv()
     rows[...] = jnp.zeros_like(rows)
-    last = gath[:, 0, :]
-    fwd.fill(last)
-    bwd.fill(last)
-    turned = jnp.transpose(rows[...])
-    for r in range(2 * (6 + 3 * steps)):
-        coef[r] = jnp.broadcast_to(turned[:heads, r : r + 1], (heads, LANES))
-
-    def rest(k, carry):
-        guarded(k, states)
-        fwd.combine(k - LEAD)
-        return carry
-
-    lax.fori_loop(LEAD, half + LEAD, rest, 0)
-    acc_s[...] = jnp.zeros_like(acc_s)
-    acc_p[...] = jnp.zeros_like(acc_p)
+    mine, other = gath[me, 0:1, :], gath[mate, 0:1, :]
+    fwd.fill_near(mine, other)
+    bwd.fill_near(mine, other)
+
+    def spread_rows(picked):
+        turned = jnp.transpose(rows[...])
+        for r in picked:
+            coef[r] = jnp.broadcast_to(turned[:heads, r : r + 1], (heads, LANES))
+
+    near = [scan.base + row for scan in (fwd, bwd) for row in range(4)]
+    spread_rows(near)
+    columns_wait(k_hbm, k_ref, head_start, half, 6)
+    columns_wait(v_hbm, v_ref, head_start, half, 7)
+    for i in (1, 2, 3):
+        fetch[i].start()
+    unit = 2 if half % 2 == 0 else 1
+    count = half // unit
+    ahead = (half + LEAD - SOLO) // 2 if unit == 2 and half > SOLO else 0
+
+    def group(base):
+        return [base + i for i in range(unit)]
+
+    def feed(scan, produce, local, ready):
+        def alone(k, carry):
+            guarded(k, produce)
+            guarded(k - LEAD, scan.combine)
+            return carry
+
+        def paired(j, carry):
+            for i in range(2):
+                k = SOLO + 2 * j + i
+                guarded(k, produce)
+                guarded(k - LEAD, scan.combine)
+            local(group(core * half + 2 * j))
+            return carry
+
+        lax.fori_loop(scan.begun, SOLO if ahead else half + LEAD, alone, 0)
+        ready()
+        lax.fori_loop(0, ahead, paired, 0)
 
     def intra(hs):
         made = []
@@ -387,6 +433,21 @@
         for h, w, a in made:
             fw[h] = w
             att[:, lanes(h)] = a
+
+    fwd.begun, bwd.begun = LEAD, 0
+
+    def ready():
+        for i in (1, 2, 3):
+            fetch[i].wait()
+
+    feed(fwd, states, intra, ready)
+    gather_all().wait_recv()
+    last = gath[:, 0, :]
+    fwd.fill(last)
+    bwd.fill(last)
+    spread_rows([r for r in range(2 * (6 + 3 * steps)) if r not in near])
+    acc_s[...] = jnp.zeros_like(acc_s)
+    acc_p[...] = jnp.zeros_like(acc_p)
 
     def scaled_of(h):
         return gain_ref[:, lanes(h)] * g_ref[:, lanes(h)].astype(F32)
@@ -404,14 +465,9 @@
         for h, a, p in made:
             att[:, lanes(h)] = a
 
-    unit = 2 if half % 2 == 0 else 1
-    count = half // unit
     spread = -(-LAG // unit)
     lags = [0, count] if steps == 2 else [spread * s for s in range(steps)]
     lag_in = max(lags[-1] + spread, count)
-
-    def group(base):
-        return [base + i for i in range(unit)]
 
     def pass_loop(scan, local, finish, extra=None):
         def one(it, carry):
@@ -423,11 +479,13 @@
                     for k in group(at * unit):
                         scan.step(s, k)
 
-            @pl.when(it < 2 * count)
-            def _():
-                late = it // count
+            turn = it + ahead
+
+            @pl.when(turn < 2 * count)
+            def _():
+                late = turn // count
                 who = core + late * (1 - 2 * core)
-                local(group(who * half + (it - late * count) * unit))
+                local(group(who * half + (turn - late * count) * unit))
 
             if extra is not None:
                 extra(it)
@@ -450,8 +508,6 @@
 
         lax.fori_loop(0, count + lag_in, one, 0)
 
-    loads[2].wait()
-    loads[3].wait()
     pass_loop(fwd, intra, inter)
 
     mean_sq = jnp.sum(acc_s[...], axis=1, keepdims=True) * (1.0 / feat)
@@ -481,66 +537,6 @@
         keep_delta(far)
         bwd.die1(k).start()
         keep_delta(near)
-
-    def back(k, carry):
-        guarded(k, deltas)
-        guarded(k - LEAD, bwd.combine)
-        return carry
-
-    lax.fori_loop(0, half + LEAD, back, 0)
-
-    part = feat // n_dp
-
-    def gain_in():
-        return remote(gp, gx.at[me], gx_s, gx_r, context=lead_of)
-
-    def gain_in_all():
-        span = gx.at[pl.ds(0, n - 1)]
-        return remote(span, span, gx_s, gx_r, context=lead_of - 1)
-
-    def gain_across(r):
-        to = (dp + r) % n_dp
-        return remote(gp.at[:, pl.ds(pl.multiple_of(to * part, LANES), part)], gz.at[r], gy_s, gy_r, dp=to)
-
-    def gain_across_all():
-        span = gz.at[pl.ds(1, n_dp - 1)]
-        return remote(span, span, gy_s, gy_r, dp=(dp + 1) % n_dp)
-
-    def gain_out(i):
-        return remote(gy.at[i], gy.at[lead_of], gz_s, gz_r, context=i)
-
-    def gain_out_all():
-        span = gy.at[pl.ds(0, n - 1)]
-        return remote(span, span, gz_s, gz_r, context=lead_of - 1)
-
-    @pl.when(jnp.logical_not(leads))
-    def _():
-        gain_in().start()
-
-    def gain_step(it):
-        @pl.when(leads & (it == count // 2))
-        def _():
-            gain_in_all().wait_recv()
-            total = gp[...]
-            for r in range(n - 1):
-                total = total + gx[r]
-            gp[...] = total
-            if n_dp > 1:
-                pl.semaphore_wait(barrier, n_dp - 1)
-                for r in range(1, n_dp):
-                    gain_across(r).start()
-
-        @pl.when(leads & (it == count))
-        def _():
-            total = gp[:, pl.ds(pl.multiple_of(dp * part, LANES), part)]
-            if n_dp > 1:
-                gain_across_all().wait_recv()
-                for r in range(1, n_dp):
-                    total = total + gz[r]
-            for i in range(n):
-                gy[i] = jnp.broadcast_to(total[:, i * width : (i + 1) * width], (8, width))
-            for i in range(n - 1):
-                gain_out(i).start()
 
     def local_back(hs):
         made = []
@@ -557,6 +553,61 @@
             att[:, lanes(h)] = kl
             vloc[:, lanes(h)] = vl
 
+    feed(bwd, deltas, local_back, lambda: None)
+
+    part = feat // n_dp
+
+    def gain_in():
+        return remote(gp, gx.at[me], gx_s, gx_r, context=lead_of)
+
+    def gain_in_all():
+        span = gx.at[pl.ds(0, n - 1)]
+        return remote(span, span, gx_s, gx_r, context=lead_of - 1)
+
+    def gain_across(r):
+        to = (dp + r) % n_dp
+        return remote(gp.at[:, pl.ds(pl.multiple_of(to * part, LANES), part)], gz.at[r], gy_s, gy_r, dp=to)
+
+    def gain_across_all():
+        span = gz.at[pl.ds(1, n_dp - 1)]
+        return remote(span, span, gy_s, gy_r, dp=(dp + 1) % n_dp)
+
+    def gain_out(i):
+        return remote(gy.at[i], gy.at[lead_of], gz_s, gz_r, context=i)
+
+    def gain_out_all():
+        span = gy.at[pl.ds(0, n - 1)]
+        return remote(span, span, gz_s, gz_r, context=lead_of - 1)
+
+    @pl.when(jnp.logical_not(leads))
+    def _():
+        gain_in().start()
+
+    def gain_step(it):
+        @pl.when(leads & (it == count // 2))
+        def _():
+            gain_in_all().wait_recv()
+            total = gp[...]
+            for r in range(n - 1):
+                total = total + gx[r]
+            gp[...] = total
+            if n_dp > 1:
+                pl.semaphore_wait(barrier, n_dp - 1)
+                for r in range(1, n_dp):
+                    gain_across(r).start()
+
+        @pl.when(leads & (it == count))
+        def _():
+            total = gp[:, pl.ds(pl.multiple_of(dp * part, LANES), part)]
+            if n_dp > 1:
+                gain_across_all().wait_recv()
+                for r in range(1, n_dp):
+                    total = total + gz[r]
+            for i in range(n):
+                gy[i] = jnp.broadcast_to(total[:, i * width : (i + 1) * width], (8, width))
+            for i in range(n - 1):
+                gain_out(i).start()
+
     def finish_back(hs):
         made = []
         for h in hs:
@@ -583,6 +634,7 @@
             gain_across_all().wait_send()
 
     gg_ref[...] = gy[lead_of][0:1, :] * cfg["norm"]
+    gather_mate().wait_send()
     gather_all().wait_send()
     fwd.drain()
     bwd.drain()
@@ -637,7 +689,7 @@
 
     rows_bf = pltpu.VMEM((pos, feat), BF16)
     scratch = [
-        *([rows_bf] * 4), sem((4,)),
+        *([rows_bf] * 4), pltpu.VMEM((heads, pos), F32), pltpu.VMEM((1, feat), F32), sem((8,)),
         pltpu.VMEM((pos, LANES), F32),
         pltpu.VMEM((LANES, pos), F32),
         pltpu.VMEM((heads, pos, LANES), F32),
@@ -656,7 +708,7 @@
         pltpu.VMEM((n_dp, 1, feat // n_dp), F32),
         *scan_buffers(),
         *scan_buffers(),
-        pltpu.SemaphoreType.REGULAR(()), *[sem(())] * 8,
+        pltpu.SemaphoreType.REGULAR(()), *[sem(())] * 10,
         *scan_sems(),
         *[scan_sems()[i] for i in (0, 2, 3, 4)],
     ]
@@ -665,7 +717,7 @@
     qg, kg, vg, gg = pl.pallas_call(
         functools.partial(body, cfg),
         out_shape=(grid_out, grid_out, grid_out, pltpu.VMEM((1, width), F32)),
-        in_specs=[pl.BlockSpec(memory_space=pl.ANY)] * 4 + [vmem] * 2,
+        in_specs=[pl.BlockSpec(memory_space=pl.ANY)] * 6,
         out_specs=(vmem,) * 4,
         scratch_shapes=scratch,
         compiler_params=pltpu.CompilerParams(

time: 66.4 us -> 63 us (0.949)
  Pallas kernels: 65.5 us -> 62.1 us
    pallas_call x1, Pallas kernels: 63.3 us -> 59.9 us  [per_device(): pl.pallas_call(functools.partial(body, cfg), out_shape=(grid_out, grid_ou...]
where the time goes in v5:
time: 63 us; the launch traced here: 62.8 us
  Pallas kernels  62.1 us (99%)
  between operations  0.64 us (1%)
    pallas_call x1, Pallas kernels, per_device(): pl.pallas_call(functools.partial(body, cfg), out_shape=(grid_out, grid_ou...  59.9 us
    pallas_call x1, Pallas kernels, settled(): pl.pallas_call(functools.partial(settle, count), out_shape=tuple((jax.Sha...  2.22 us

profile of v5, /device:TPU:0, one launch (start us, length us, event | category | flops | bytes accessed | tf_op | source)
XLA Modules:
  0.0 62.8 jit_solution(1936368806144239490)
XLA Ops:
  0.6 59.9 %shard_map.93 = (bf16[192,4096]{1,0:T(8,128)(2,1)S(1)}, bf16[192,4096]{1,0:T(8,128)(2,1)S(1)}, bf16[192,4096]{1,0:T(8,128)(2,1)S(1)}, f32[1,128]{1,0:T(1,128)S(1)}) custom-call(bf16[192,4096]{1,0:T(8,128)(2,1)} %bitcast.12, bf16[192,4096]{1,0:T(8,128)(2,1)} %bitcast.13, bf16[192,4096]{1,0:T(8,128)(2,1)} %bitcast.14, bf16[192,4096]{1,0:T(8,128)(2,1)} %bitcast.15, ...), custom_call_target="tpu_custom_call" | custom-call | tf_op jit(solution)/shard_map/pallas_call | solution.py:717
  60.6 2.2 %shard_map.94 = (bf16[192,4096]{1,0:T(8,128)(2,1)}, bf16[192,4096]{1,0:T(8,128)(2,1)}, bf16[192,4096]{1,0:T(8,128)(2,1)}, f32[1,128]{1,0:T(1,128)}) custom-call(bf16[192,4096]{1,0:T(8,128)(2,1)S(1)} %get-tuple-element.12.refs_0_, bf16[192,4096]{1,0:T(8,128)(2,1)S(1)} %get-tuple-element.13.refs_1_, bf16[192,4096]{1,0:T(8,128)(2,1)S(1)} %get-tuple-element.14.refs_2_, ...), custom_call_target="tpu_custom_call" | custom-call | tf_op jit(solution)/shard_map/pallas_call | solution.py:654

commit v6 on v5

--- a/solution.py
+++ b/solution.py
@@ -14,7 +14,7 @@
 LANES = 128
 LAG = 2
 LEAD = 2
-SOLO = 6
+SOLO = 8
 
 
 def dot_nn(a, b):
@@ -39,11 +39,13 @@
     st_f, pr_f, tot_f, rx_f, sd_f, inc, pf_f,
     st_b, pr_b, tot_b, rx_b, sd_b, later, pf_b,
     entry, gm_s, gm_r, ga_s, ga_r, gx_s, gx_r, gy_s, gy_r, gz_s, gz_r,
-    d1s_f, d1r_f, xs_f, xr_f, d2s_f, d2r_f,
-    d1s_b, xs_b, xr_b, d2s_b,
+    d1s_f, d1r_f, xs_f, xr_f, xe_f, d2s_f, d2r_f,
+    d1s_b, xs_b, xr_b, xe_b, d2s_b,
 ):
     n, n_dp, steps, heads = cfg["n"], cfg["n_dp"], cfg["steps"], cfg["heads"]
     half = heads // 2
+    unit = 2 if half % 2 == 0 else 1
+    count = half // unit
     pos = q_ref.shape[0]
     feat = q_ref.shape[1]
     size = feat // heads
@@ -157,9 +159,9 @@
         return jnp.exp(jnp.where(row_i >= col_i, wide - cum_t[pl.ds(h, 1), :], -jnp.inf))
 
     class Scan:
-        def __init__(self, forward, st, pr, tot, rx, sd, result, pf, d1s, d1r, xs, xr, d2s, d2r):
+        def __init__(self, forward, st, pr, tot, rx, sd, result, pf, d1s, d1r, xs, xr, xe, d2s, d2r):
             self.forward, self.st, self.pr, self.tot, self.rx = forward, st, pr, tot, rx
-            self.sd, self.result, self.pf = sd, result, pf
+            self.sd, self.result, self.pf, self.xe = sd, result, pf, xe
             self.d1s, self.d1r, self.xs, self.xr, self.d2s, self.d2r = d1s, d1r, xs, xr, d2s, d2r
             self.first = (core == 0) if forward else (core == 1)
             self.base = 0 if forward else 6 + 3 * steps
@@ -210,19 +212,22 @@
         def die1(self, k):
             return remote(self.st.at[(1 - core) * half + k], self.pr.at[k], self.d1s, self.d1r.at[k], context=mate)
 
-        def link(self, s, k, slot=None):
+        def link(self, s, k, slot=None, own=None):
+            if steps == 2 and s == 0 and slot is None:
+                own = self.xe.at[k // 2]
             group = self.xs.at[steps if slot == 1 else s]
-            return remote(self.tot.at[s if slot is None else slot, k], self.rx.at[s, k], group, self.xr.at[s, k], context=self.partner[s])
+            return remote(self.tot.at[s if slot is None else slot, k], self.rx.at[s, k], group, self.xr.at[s, k] if own is None else own, context=self.partner[s])
 
         def sent(self, group, count):
             span = self.rx.at[0, pl.ds(0, count)]
-            return remote(span, span, self.xs.at[group], self.xr.at[0, 0], context=mate)
+            return remote(span, span, self.xs.at[group], self.d2r.at[0], context=mate)
 
         def die2(self, k):
-            return remote(self.sd.at[k], self.result.at[core * half + k], self.d2s, self.d2r.at[k], context=mate)
-
-        def die2_in(self, k):
-            return remote(self.sd.at[k], self.result.at[(1 - core) * half + k], self.d2s, self.d2r.at[k], context=mate)
+            return remote(self.sd.at[k], self.result.at[core * half + k], self.d2s, self.d2r.at[k // unit], context=mate)
+
+        def die2_in(self, base):
+            span = self.sd.at[pl.ds(0, unit)]
+            return remote(span, span, self.d2s, self.d2r.at[base // unit], context=mate)
 
         def send(self, s, k):
             if s < steps - 1:
@@ -237,7 +242,7 @@
                 self.send(0, k)
                 return
 
-            @pl.when(k % 2 == 0)
+            @pl.when((k % 2 == 0) & (self.ups[0] | self.ups[1]))
             def _():
                 self.send(0, k)
 
@@ -254,11 +259,15 @@
             down0, down1 = jnp.logical_not(up0), jnp.logical_not(up1)
             even, odd = k % 2 == 0, k % 2 == 1
 
-            @pl.when(even)
-            def _():
-                self.stage(s, k)
-
             if s == 0:
+                @pl.when(even & (down0 | up1))
+                def _():
+                    self.stage(s, k)
+
+                @pl.when(even & up0 & down1)
+                def _():
+                    self.pf[k] = jnp.zeros_like(self.pf[k])
+
                 @pl.when(odd & up1 & up0)
                 def _():
                     self.tot[1, k] = self.tot[0, k]
@@ -280,6 +289,10 @@
                 def _():
                     self.link(0, k, 1).start()
             else:
+                @pl.when(even)
+                def _():
+                    self.stage(s, k)
+
                 @pl.when(odd & (down0 | down1))
                 def _():
                     self.link(0, k, 1).wait_recv()
@@ -339,7 +352,10 @@
                     self.sent(steps - 1, half).wait_send()
 
                 return
-            self.sent(0, half // 2).wait_send()
+
+            @pl.when(self.ups[0] | self.ups[1])
+            def _():
+                self.sent(0, half // 2).wait_send()
 
             @pl.when(self.ups[1])
             def _():
@@ -349,8 +365,8 @@
             def _():
                 self.sent(2, half // 2).wait_send()
 
-    fwd = Scan(True, st_f, pr_f, tot_f, rx_f, sd_f, inc, pf_f, d1s_f, d1r_f, xs_f, xr_f, d2s_f, d2r_f)
-    bwd = Scan(False, st_b, pr_b, tot_b, rx_b, sd_b, later, pf_b, d1s_b, d1r_f, xs_b, xr_b, d2s_b, d2r_f)
+    fwd = Scan(True, st_f, pr_f, tot_f, rx_f, sd_f, inc, pf_f, d1s_f, d1r_f, xs_f, xr_f, xe_f, d2s_f, d2r_f)
+    bwd = Scan(False, st_b, pr_b, tot_b, rx_b, sd_b, later, pf_b, d1s_b, d1r_f, xs_b, xr_f if steps == 2 else xr_b, xe_b, d2s_b, d2r_f)
 
     def guarded(k, run):
         @pl.when((k >= 0) & (k < half))
@@ -399,30 +415,27 @@
     columns_wait(v_hbm, v_ref, head_start, half, 7)
     for i in (1, 2, 3):
         fetch[i].start()
-    unit = 2 if half % 2 == 0 else 1
-    count = half // unit
     ahead = (half + LEAD - SOLO) // 2 if unit == 2 and half > SOLO else 0
 
     def group(base):
         return [base + i for i in range(unit)]
 
     def feed(scan, produce, local, ready):
-        def alone(k, carry):
+        def one(k, carry):
             guarded(k, produce)
             guarded(k - LEAD, scan.combine)
+            if ahead:
+                pl.when(k == SOLO)(ready)
+
+                @pl.when((k > SOLO) & ((k - SOLO) % 2 == 1))
+                def _():
+                    local(group(core * half + k - SOLO - 1))
+
             return carry
 
-        def paired(j, carry):
-            for i in range(2):
-                k = SOLO + 2 * j + i
-                guarded(k, produce)
-                guarded(k - LEAD, scan.combine)
-            local(group(core * half + 2 * j))
-            return carry
-
-        lax.fori_loop(scan.begun, SOLO if ahead else half + LEAD, alone, 0)
-        ready()
-        lax.fori_loop(0, ahead, paired, 0)
+        lax.fori_loop(scan.begun, half + LEAD, one, 0)
+        if not ahead:
+            ready()
 
     def intra(hs):
         made = []
@@ -500,8 +513,7 @@
 
             @pl.when((come >= 0) & (come < count))
             def _():
-                for k in group(come * unit):
-                    scan.die2_in(k).wait_recv()
+                scan.die2_in(come * unit).wait_recv()
                 finish(group((1 - core) * half + come * unit))
 
             return carry
@@ -584,7 +596,7 @@
         gain_in().start()
 
     def gain_step(it):
-        @pl.when(leads & (it == count // 2))
+        @pl.when(leads & (it == count))
         def _():
             gain_in_all().wait_recv()
             total = gp[...]
@@ -596,7 +608,7 @@
                 for r in range(1, n_dp):
                     gain_across(r).start()
 
-        @pl.when(leads & (it == count))
+        @pl.when(leads & (it == 2 * count - 2))
         def _():
             total = gp[:, pl.ds(pl.multiple_of(dp * part, LANES), part)]
             if n_dp > 1:
@@ -685,7 +697,13 @@
         ]
 
     def scan_sems():
-        return [sem(()), sem((half,)), sem((steps + 1,)), sem((steps, half)), sem(()), sem((half,))]
+        evens = half // 2 if steps == 2 else 1
+        odd_first = sem((steps, half))
+        return [sem(()), sem((half,)), sem((steps + 1,)), odd_first, sem((evens,)), sem(()), sem((half // 2 if half % 2 == 0 else half,))]
+
+    def scan_sems_more():
+        first = scan_sems()
+        return [first[0], first[2], sem((1, 1)) if steps == 2 else first[3], first[4], first[5]]
 
     rows_bf = pltpu.VMEM((pos, feat), BF16)
     scratch = [
@@ -710,7 +728,7 @@
         *scan_buffers(),
         pltpu.SemaphoreType.REGULAR(()), *[sem(())] * 10,
         *scan_sems(),
-        *[scan_sems()[i] for i in (0, 2, 3, 4)],
+        *scan_sems_more(),
     ]
     grid_out = pltpu.VMEM((pos, feat), BF16)
     spare = 3 * pos * feat * 2 + (1 << 20)

time: 63 us -> 62.8 us (level)
  no operation moved by 1% of the time
where the time goes in v6:
time: 62.8 us; the launch traced here: 62.6 us
  Pallas kernels  62 us (99%)
  between operations  0.64 us (1%)
    pallas_call x1, Pallas kernels, per_device(): pl.pallas_call(functools.partial(body, cfg), out_shape=(grid_out, grid_ou...  59.8 us
    pallas_call x1, Pallas kernels, settled(): pl.pallas_call(functools.partial(settle, count), out_shape=tuple((jax.Sha...  2.22 us

profile of v6, /device:TPU:0, one launch (start us, length us, event | category | flops | bytes accessed | tf_op | source)
XLA Modules:
  0.0 62.6 jit_solution(6692218405489231918)
XLA Ops:
  0.6 59.8 %shard_map.93 = (bf16[192,4096]{1,0:T(8,128)(2,1)S(1)}, bf16[192,4096]{1,0:T(8,128)(2,1)S(1)}, bf16[192,4096]{1,0:T(8,128)(2,1)S(1)}, f32[1,128]{1,0:T(1,128)S(1)}) custom-call(bf16[192,4096]{1,0:T(8,128)(2,1)} %bitcast.12, bf16[192,4096]{1,0:T(8,128)(2,1)} %bitcast.13, bf16[192,4096]{1,0:T(8,128)(2,1)} %bitcast.14, bf16[192,4096]{1,0:T(8,128)(2,1)} %bitcast.15, ...), custom_call_target="tpu_custom_call" | custom-call | tf_op jit(solution)/shard_map/pallas_call | solution.py:735
  60.4 2.2 %shard_map.94 = (bf16[192,4096]{1,0:T(8,128)(2,1)}, bf16[192,4096]{1,0:T(8,128)(2,1)}, bf16[192,4096]{1,0:T(8,128)(2,1)}, f32[1,128]{1,0:T(1,128)}) custom-call(bf16[192,4096]{1,0:T(8,128)(2,1)S(1)} %get-tuple-element.12.refs_0_, bf16[192,4096]{1,0:T(8,128)(2,1)S(1)} %get-tuple-element.13.refs_1_, bf16[192,4096]{1,0:T(8,128)(2,1)S(1)} %get-tuple-element.14.refs_2_, ...), custom_call_target="tpu_custom_call" | custom-call | tf_op jit(solution)/shard_map/pallas_call | solution.py:666

commit v7 on v6

--- a/solution.py
+++ b/solution.py
@@ -46,6 +46,7 @@
     half = heads // 2
     unit = 2 if half % 2 == 0 else 1
     count = half // unit
+    near_ring, back_ring = cfg["near_ring"], cfg["back_ring"]
     pos = q_ref.shape[0]
     feat = q_ref.shape[1]
     size = feat // heads
@@ -210,11 +211,13 @@
                 put(5 + 3 * steps, between(far, near))
 
         def die1(self, k):
-            return remote(self.st.at[(1 - core) * half + k], self.pr.at[k], self.d1s, self.d1r.at[k], context=mate)
+            return remote(self.st.at[(1 - core) * half + k], self.pr.at[k], self.d1s, self.d1r.at[k % near_ring], context=mate)
 
         def link(self, s, k, slot=None, own=None):
             if steps == 2 and s == 0 and slot is None:
                 own = self.xe.at[k // 2]
+            elif steps == 2:
+                own = self.xr.at[{(0, 1): 0, (1, None): 1, (1, 0): 2}[s, slot], k // 2]
             group = self.xs.at[steps if slot == 1 else s]
             return remote(self.tot.at[s if slot is None else slot, k], self.rx.at[s, k], group, self.xr.at[s, k] if own is None else own, context=self.partner[s])
 
@@ -223,11 +226,11 @@
             return remote(span, span, self.xs.at[group], self.d2r.at[0], context=mate)
 
         def die2(self, k):
-            return remote(self.sd.at[k], self.result.at[core * half + k], self.d2s, self.d2r.at[k // unit], context=mate)
+            return remote(self.sd.at[k], self.result.at[core * half + k], self.d2s, self.d2r.at[(k // unit) % back_ring], context=mate)
 
         def die2_in(self, base):
             span = self.sd.at[pl.ds(0, unit)]
-            return remote(span, span, self.d2s, self.d2r.at[base // unit], context=mate)
+            return remote(span, span, self.d2s, self.d2r.at[(base // unit) % back_ring], context=mate)
 
         def send(self, s, k):
             if s < steps - 1:
@@ -681,7 +684,10 @@
     n, n_dp = lax.axis_size("context"), lax.axis_size("dp")
     steps = (n // 2).bit_length() - 1
     width = feat // (n * n_dp)
-    cfg = dict(n=n, n_dp=n_dp, steps=steps, heads=heads, norm=1.0 / math.sqrt(pos * n * n_dp))
+    pairs = half // 2 if half % 2 == 0 else half
+    near_ring = 8 if half % 8 == 0 else half
+    back_ring = 4 if steps == 2 and pairs % 4 == 0 else pairs
+    cfg = dict(near_ring=near_ring, back_ring=back_ring, n=n, n_dp=n_dp, steps=steps, heads=heads, norm=1.0 / math.sqrt(pos * n * n_dp))
     vmem = pl.BlockSpec(memory_space=pltpu.VMEM)
     sem = pltpu.SemaphoreType.DMA
 
@@ -698,8 +704,8 @@
 
     def scan_sems():
         evens = half // 2 if steps == 2 else 1
-        odd_first = sem((steps, half))
-        return [sem(()), sem((half,)), sem((steps + 1,)), odd_first, sem((evens,)), sem(()), sem((half // 2 if half % 2 == 0 else half,))]
+        links = sem((3, half // 2)) if steps == 2 else sem((steps, half))
+        return [sem(()), sem((near_ring,)), sem((steps + 1,)), links, sem((evens,)), sem(()), sem((back_ring,))]
 
     def scan_sems_more():
         first = scan_sems()
@@ -721,7 +727,7 @@
         pltpu.VMEM((LANES, LANES), F32),
         pltpu.VMEM((2 * (6 + 3 * steps), heads, LANES), F32),
         pltpu.VMEM((1, feat), F32),
-        pltpu.VMEM((n - 1, 1, feat), F32),
+        pltpu.VMEM((n, 1, feat), F32),
         pltpu.VMEM((n, 8, width), F32),
         pltpu.VMEM((n_dp, 1, feat // n_dp), F32),
         *scan_buffers(),

time: 62.8 us -> 62.7 us (level)
  no operation moved by 1% of the time
where the time goes in v7:
time: 62.7 us; the launch traced here: 62.4 us
  Pallas kernels  61.8 us (99%)
  between operations  0.64 us (1%)
    pallas_call x1, Pallas kernels, per_device(): pl.pallas_call(functools.partial(body, cfg), out_shape=(grid_out, grid_ou...  59.6 us
    pallas_call x1, Pallas kernels, settled(): pl.pallas_call(functools.partial(settle, count), out_shape=tuple((jax.Sha...  2.22 us

profile of v7, /device:TPU:0, one launch (start us, length us, event | category | flops | bytes accessed | tf_op | source)
XLA Modules:
  0.0 62.4 jit_solution(6665500567006399751)
XLA Ops:
  0.6 59.6 %shard_map.93 = (bf16[192,4096]{1,0:T(8,128)(2,1)S(1)}, bf16[192,4096]{1,0:T(8,128)(2,1)S(1)}, bf16[192,4096]{1,0:T(8,128)(2,1)S(1)}, f32[1,128]{1,0:T(1,128)S(1)}) custom-call(bf16[192,4096]{1,0:T(8,128)(2,1)} %bitcast.12, bf16[192,4096]{1,0:T(8,128)(2,1)} %bitcast.13, bf16[192,4096]{1,0:T(8,128)(2,1)} %bitcast.14, bf16[192,4096]{1,0:T(8,128)(2,1)} %bitcast.15, ...), custom_call_target="tpu_custom_call" | custom-call | tf_op jit(solution)/shard_map/pallas_call | solution.py:741
  60.2 2.2 %shard_map.94 = (bf16[192,4096]{1,0:T(8,128)(2,1)}, bf16[192,4096]{1,0:T(8,128)(2,1)}, bf16[192,4096]{1,0:T(8,128)(2,1)}, f32[1,128]{1,0:T(1,128)}) custom-call(bf16[192,4096]{1,0:T(8,128)(2,1)S(1)} %get-tuple-element.12.refs_0_, bf16[192,4096]{1,0:T(8,128)(2,1)S(1)} %get-tuple-element.13.refs_1_, bf16[192,4096]{1,0:T(8,128)(2,1)S(1)} %get-tuple-element.14.refs_2_, ...), custom_call_target="tpu_custom_call" | custom-call | tf_op jit(solution)/shard_map/pallas_call | solution.py:669

commit v8 on v7

--- a/solution.py
+++ b/solution.py
@@ -416,8 +416,6 @@
     spread_rows(near)
     columns_wait(k_hbm, k_ref, head_start, half, 6)
     columns_wait(v_hbm, v_ref, head_start, half, 7)
-    for i in (1, 2, 3):
-        fetch[i].start()
     ahead = (half + LEAD - SOLO) // 2 if unit == 2 and half > SOLO else 0
 
     def group(base):
@@ -427,6 +425,12 @@
         def one(k, carry):
             guarded(k, produce)
             guarded(k - LEAD, scan.combine)
+            if scan.forward:
+                @pl.when(k == LEAD + 1)
+                def _():
+                    for i in (1, 2, 3):
+                        fetch[i].start()
+
             if ahead:
                 pl.when(k == SOLO)(ready)
 
@@ -482,8 +486,8 @@
             att[:, lanes(h)] = a
 
     spread = -(-LAG // unit)
-    lags = [0, count] if steps == 2 else [spread * s for s in range(steps)]
-    lag_in = max(lags[-1] + spread, count)
+    lags = [0, max(count - 2, spread)] if steps == 2 else [spread * s for s in range(steps)]
+    lag_in = max(lags[-1] + spread, count - ahead)
 
     def pass_loop(scan, local, finish, extra=None):
         def one(it, carry):
@@ -611,7 +615,7 @@
                 for r in range(1, n_dp):
                     gain_across(r).start()
 
-        @pl.when(leads & (it == 2 * count - 2))
+        @pl.when(leads & (it == count + lag_in - 2))
         def _():
             total = gp[:, pl.ds(pl.multiple_of(dp * part, LANES), part)]
             if n_dp > 1:
@@ -657,11 +661,14 @@
 
 def settle(count, *refs):
     srcs, dsts, sems = refs[:count], refs[count : 2 * count], refs[2 * count]
-    copies = [pltpu.make_async_copy(srcs[i], dsts[i], sems.at[i]) for i in range(count)]
-    for copy in copies:
-        copy.start()
-    for copy in copies:
-        copy.wait()
+    for i in range(count):
+        rows = srcs[i].shape[0]
+        parts = 4 if rows % 64 == 0 else 1
+        for j in range(parts):
+            at = pl.ds(j * (rows // parts), rows // parts)
+            pltpu.make_async_copy(srcs[i].at[at], dsts[i].at[at], sems.at[i]).start()
+    for i in range(count):
+        pltpu.make_async_copy(srcs[i], dsts[i], sems.at[i]).wait()
 
 
 def settled(arrays):

time: 62.7 us -> 62.7 us (level)
  no operation moved by 1% of the time
where the time goes in v8:
time: 62.7 us; the launch traced here: 62.4 us
  Pallas kernels  61.8 us (99%)
  between operations  0.64 us (1%)
    pallas_call x1, Pallas kernels, per_device(): pl.pallas_call(functools.partial(body, cfg), out_shape=(grid_out, grid_ou...  59.6 us
    pallas_call x1, Pallas kernels, settled(): pl.pallas_call(functools.partial(settle, count), out_shape=tuple((jax.Sha...  2.21 us

profile of v8, /device:TPU:0, one launch (start us, length us, event | category | flops | bytes accessed | tf_op | source)
XLA Modules:
  0.0 62.4 jit_solution(15101880351293889234)
XLA Ops:
  0.6 59.6 %shard_map.93 = (bf16[192,4096]{1,0:T(8,128)(2,1)S(1)}, bf16[192,4096]{1,0:T(8,128)(2,1)S(1)}, bf16[192,4096]{1,0:T(8,128)(2,1)S(1)}, f32[1,128]{1,0:T(1,128)S(1)}) custom-call(bf16[192,4096]{1,0:T(8,128)(2,1)} %bitcast.12, bf16[192,4096]{1,0:T(8,128)(2,1)} %bitcast.13, bf16[192,4096]{1,0:T(8,128)(2,1)} %bitcast.14, bf16[192,4096]{1,0:T(8,128)(2,1)} %bitcast.15, ...), custom_call_target="tpu_custom_call" | custom-call | tf_op jit(solution)/shard_map/pallas_call | solution.py:748
  60.2 2.2 %shard_map.94 = (bf16[192,4096]{1,0:T(8,128)(2,1)}, bf16[192,4096]{1,0:T(8,128)(2,1)}, bf16[192,4096]{1,0:T(8,128)(2,1)}, f32[1,128]{1,0:T(1,128)}) custom-call(bf16[192,4096]{1,0:T(8,128)(2,1)S(1)} %get-tuple-element.12.refs_0_, bf16[192,4096]{1,0:T(8,128)(2,1)S(1)} %get-tuple-element.13.refs_1_, bf16[192,4096]{1,0:T(8,128)(2,1)S(1)} %get-tuple-element.14.refs_2_, ...), custom_call_target="tpu_custom_call" | custom-call | tf_op jit(solution)/shard_map/pallas_call | solution.py:676
